TPU v7x, 128 devices: a whole 4x4x4 slice. The times are simulated.
128 devices in a mesh: dp: 16 (over x, z_hi, core), tm: 8 (over z_lo, y).
Axes of the slice: x: 4, y: 4, z: 4 (z_hi: 2, z_lo: 2; z = z_hi * 2 + z_lo), core: 2. Of those that a mesh axis runs over, the one named last changes fastest.
Arguments:
- loaded: bfloat16 [16, 64, 16, 16, 256], P('dp', 'tm')
- lengths: int32 [16, 8], P('dp'), may hold values from 1 to 8, as said below
- resolution: int32 [16, 2], P('dp'), may hold values from 8 to 16, as said below
- weight: bfloat16 [27, 256, 256], replicated, may hold values from -0.078125 to 0.078125
- norm_gain: float32 [256], replicated, may hold values from 0.1 to 1.9
- norm_bias: float32 [256], replicated, may hold values from -3 to 3
- cotangent: bfloat16 [16, 64, 16, 16, 256], P('dp', 'tm'), may hold values from -6 to 6
Outputs:
- encoded: bfloat16 [16, 64, 16, 16, 256], P('dp', 'tm')
- input_grad: bfloat16 [16, 64, 16, 16, 256], P('dp', 'tm')
- weight_grad: float32 [27, 256, 256], replicated
- gain_grad: float32 [256], replicated
- bias_grad: float32 [256], replicated
Inputs may be any that keep to these rules, and one draw needn't show every extreme that they name: `lengths`: row c lists how many consecutive frames of clip c each index of tm loaded, in frame order; the row sums to the clip's frame count, which is 64 - k for some 0 <= k <= 8, so that every loaded frame belongs to the loader's own temporal slab or to the one before it; in every draw one clip has all 64 frames, 8 on every index. `resolution`: valid rows (column 0) and columns (column 1) of clip c; frames are padded at the bottom and right; at least 8 rows and 8 columns, and in every draw one clip has the full 16 by 16.
All inputs are finite; a program needn't handle non-finite values.
Results may differ from a plain program's by a relative error of at most 0.0046.
The roundings to bfloat16 on the way count: a program that leaves them out, or rounds other values in their place, can miss the bound.
Values may be sent and summed in bfloat16 or wider, within the bound.
A program may use at most 128 MiB of HBM per device.

v0:
```python
import math

import jax
import jax.numpy as jnp
from jax import lax
from jax.sharding import PartitionSpec as P

GROUPS = 32


EPSILON = 1e-05


def shifted(block, axis, distance):
    devices = range(lax.axis_size(axis))
    route = [(i - distance, i) for i in devices if i - distance in devices]
    return lax.ppermute(block, axis, route)


def group_total(values):
    shaped = values.reshape(values.shape[:-1] + (GROUPS, values.shape[-1] // GROUPS))
    return jnp.sum(shaped, axis=(0, 1, 2, 4))


def spread_groups(per_group, channels):
    return jnp.repeat(per_group, channels // per_group.shape[0])


def tap_sweeps(past_pad, future_pad, weight, frames, frame_rows, frame_cols):
    channels = weight.shape[2]
    positions = frames * frame_rows * frame_cols
    forward = jnp.zeros((positions, channels), jnp.float32)
    backward = jnp.zeros((positions, channels), jnp.float32)
    grad_flat = future_pad[:frames, 1 : frame_rows + 1, 1 : frame_cols + 1].reshape(
        positions, channels
    )
    kernel_parts = []
    for time_tap in range(3):
        for row_tap in range(3):
            for col_tap in range(3):
                tap_index = time_tap * 9 + row_tap * 3 + col_tap
                past_slice = past_pad[
                    time_tap : time_tap + frames,
                    row_tap : row_tap + frame_rows,
                    col_tap : col_tap + frame_cols,
                ].reshape(positions, channels)
                forward = forward + jnp.dot(
                    past_slice, weight[tap_index], preferred_element_type=jnp.float32
                )
                kernel_parts.append(
                    lax.dot_general(
                        past_slice,
                        grad_flat,
                        (((0,), (0,)), ((), ())),
                        preferred_element_type=jnp.float32,
                    )
                )
                future_slice = future_pad[
                    2 - time_tap : 2 - time_tap + frames,
                    2 - row_tap : 2 - row_tap + frame_rows,
                    2 - col_tap : 2 - col_tap + frame_cols,
                ].reshape(positions, channels)
                backward = backward + lax.dot_general(
                    future_slice,
                    weight[tap_index],
                    (((1,), (1,)), ((), ())),
                    preferred_element_type=jnp.float32,
                )
    return (forward, backward, jnp.stack(kernel_parts))


def place_frames(own_frames, slab_start, first_frame, own_length):
    frames = own_frames.shape[0]
    offset = slab_start + jnp.arange(frames, dtype=jnp.int32) - first_frame
    usable = (offset >= 0) & (offset < own_length)
    picked = jnp.take(own_frames, jnp.clip(offset, 0, frames - 1), axis=0)
    return picked * usable.astype(jnp.bfloat16)[:, None, None, None]


def body(loaded, lengths, resolution, weight, norm_gain, norm_bias, cotangent):
    own_frames = loaded[0]
    frames, frame_rows, frame_cols, channels = own_frames.shape
    slab_count = lax.axis_size("tm")
    own_slab = lax.axis_index("tm")
    length_row = lengths[0]
    starts = jnp.cumsum(length_row) - length_row
    frame_total = jnp.sum(length_row)
    first_frame = starts[own_slab]
    own_length = length_row[own_slab]
    staying = place_frames(own_frames, own_slab * frames, first_frame, own_length)
    leaving = place_frames(own_frames, (own_slab - 1) * frames, first_frame, own_length)
    arrived = shifted(leaving, "tm", -1)
    assembled = staying.astype(jnp.float32) + arrived.astype(jnp.float32)
    frame_ids = own_slab * frames + jnp.arange(frames, dtype=jnp.int32)
    live_rows = jnp.arange(frame_rows, dtype=jnp.int32) < resolution[0, 0]
    live_cols = jnp.arange(frame_cols, dtype=jnp.int32) < resolution[0, 1]
    live_cells = (
        (frame_ids < frame_total)[:, None, None]
        & live_rows[None, :, None]
        & live_cols[None, None, :]
    ).astype(jnp.float32)[..., None]
    inputs_f = assembled * live_cells
    cell_count = (frame_total * resolution[0, 0] * resolution[0, 1] * (channels // GROUPS)).astype(
        jnp.float32
    )
    group_means = lax.psum(group_total(inputs_f), "tm") / cell_count
    centred = (inputs_f - spread_groups(group_means, channels)) * live_cells
    variance = lax.psum(group_total(centred * centred), "tm") / cell_count
    inverse_root = spread_groups(lax.rsqrt(variance + EPSILON), channels)
    normed = centred * inverse_root
    pre_activation = normed * norm_gain + norm_bias
    gate_value = jax.nn.sigmoid(pre_activation)
    activation = (pre_activation * gate_value * live_cells).astype(jnp.bfloat16)
    earlier = shifted(activation[frames - 2 :], "tm", 1)
    past_pad = jnp.pad(
        jnp.concatenate([earlier, activation], axis=0), ((0, 0), (1, 1), (1, 1), (0, 0))
    )
    masked_grad = cotangent[0] * live_cells.astype(jnp.bfloat16)
    future = shifted(masked_grad[:2], "tm", -1)
    future_pad = jnp.pad(
        jnp.concatenate([masked_grad, future], axis=0), ((0, 0), (1, 1), (1, 1), (0, 0))
    )
    forward, backward, kernel_part = tap_sweeps(
        past_pad, future_pad, weight, frames, frame_rows, frame_cols
    )
    encoded = (forward.reshape(frames, frame_rows, frame_cols, channels) * live_cells).astype(
        jnp.bfloat16
    )
    activation_grad = backward.reshape(frames, frame_rows, frame_cols, channels) * live_cells
    pre_grad = activation_grad * gate_value * (1.0 + pre_activation * (1.0 - gate_value))
    gain_part = jnp.sum(pre_grad * normed, axis=(0, 1, 2))
    bias_part = jnp.sum(pre_grad, axis=(0, 1, 2))
    normed_grad = pre_grad * norm_gain
    normed_sum, projected_sum = lax.psum(
        (group_total(normed_grad), group_total(normed_grad * normed)), "tm"
    )
    grad_mean = spread_groups(normed_sum / cell_count, channels)
    grad_proj = spread_groups(projected_sum / cell_count, channels)
    input_grad = (
        inverse_root * (normed_grad - grad_mean - normed * grad_proj) * live_cells
    ).astype(jnp.bfloat16)
    kernel_sum, gain_sum, bias_sum = lax.psum((kernel_part, gain_part, bias_part), ("dp", "tm"))
    grad_scale = 1.0 / math.sqrt(
        lax.axis_size("dp") * slab_count * frames * frame_rows * frame_cols
    )
    return (
        encoded[None],
        input_grad[None],
        kernel_sum * grad_scale,
        gain_sum * grad_scale,
        bias_sum * grad_scale,
    )


def solution(mesh):
    placed = (
        P("dp", "tm", None, None, None),
        P("dp", None),
        P("dp", None),
        P(),
        P(),
        P(),
        P("dp", "tm", None, None, None),
    )
    return jax.shard_map(
        body,
        mesh=mesh,
        in_specs=placed,
        out_specs=(P("dp", "tm", None, None, None), P("dp", "tm", None, None, None), P(), P(), P()),
        check_vma=False,
    )
```

profile of v0, /device:TPU:1, one launch (start us, length us, event | category | flops | bytes accessed | tf_op | source)
XLA Modules:
  0.0 453.0 jit_solution(18382396377118999737)
XLA Ops:
  8.8 1.2 constant_dynamic-slice_fusion
  10.6 1.3 compare_and_fusion
  13.7 1.3 collective-permute-start
  19.5 1.3 collective-permute-start.2
  20.8 1.3 compare_and_fusion.1
  24.6 2.5 broadcast_multiply_fusion.1
  27.2 18.9 %collective-permute-done.2 = bf16[2,16,16,256]{3,2,1,0:T(8,128)(2,1)S(1)} collective-permute-done((bf16[2,16,16,256]{3,2,1,0:T(8,128)(2,1)}, bf16[2,16,16,256]{3,2,1,0:T(8,128)(2,1)S(1)}, u32[]{:S(2)}, u32[]{:S(2)}) %collective-permute-start.2) | collective-permute-done | bytes 262176 | tf_op jit(solution)/shard_map/ppermute | solution.py:17
  46.2 7.1 %pad_slice_fusion = (bf16[8,16,16,256]{3,2,1,0:T(8,128)(2,1)}, bf16[8,16,16,256]{3,2,1,0:T(8,128)(2,1)}, bf16[8,16,16,256]{3,2,1,0:T(8,128)(2,1)}, bf16[8,16,16,...) fusion(bf16[10,16,16,256]{3,2,1,0:T(8,128)(2,1)S(1)} %pad_maxim, ...), kind=kLoop, calls=%fused_computation.2 | loop fusion | bytes 21233664 | tf_op jit(solution)/shard_map/slice | solution.py:58
  53.3 2.4 pad_slice_fusion.1
  82.5 1.8 convolution_add_fusion
  84.3 1.8 fusion
  86.3 15.2 %psum.49 = f32[32]{0:T(128)S(1)} all-reduce(f32[32]{0:T(128)S(1)} %reduce_sum.76), channel_id=1, replica_groups=mesh['dp'=16,'tm'=8] {'tm'}, use_global_device_ids=true, to_apply=%region_4.6 | all-reduce | flops 32 | bytes 256 | tf_op jit(solution)/shard_map/psum | solution.py:106
  101.7 2.0 multiply_reduce_fusion.2
  103.9 25.4 %psum.50 = f32[32]{0:T(128)S(1)} all-reduce(f32[32]{0:T(128)S(1)} %reduce_sum.97), channel_id=1, replica_groups=mesh['dp'=16,'tm'=8] {'tm'}, use_global_device_ids=true, to_apply=%region_7.9 | all-reduce | flops 32 | bytes 256 | tf_op jit(solution)/shard_map/psum | solution.py:108
  129.4 4.7 %multiply_reduce_fusion = (f32[256]{0:T(256)S(1)}, f32[256]{0:T(256)S(1)}, f32[256]{0:T(256)S(1)}, f32[256]{0:T(256)S(1)}, f32[8,16,16,256]{3,2,1,0:T(8,128)}, /*index=5*/bf16[8,16,16,256]{3,2,1,0:T(8,128)(2,1)S(1)}) fusion(f32[256]{0:T(256)S(1)} %mul.181, f32[256]{0:T(256)S(1)} %sub.55, f32[8,16,16]{2,1,0:T(8,128)S(1)} %get-tuple-element.73, ...), kind=kLoop, calls=%fused_computation.103 | loop fusion | flops 15727616 | bytes 7356440 | tf_op jit(solution)/shard_map/reduce_sum | solution.py:131
  134.9 2.9 collective-permute-start.1
  138.2 15.0 %all-reduce.3 = (f32[32]{0:T(128)S(1)}, f32[32]{0:T(128)S(1)}) all-reduce(f32[32]{0:T(128)S(1)} %reduce_sum.103, f32[32]{0:T(128)S(1)} %reduce_sum.100), channel_id=1, replica_groups=mesh['dp'=16,'tm'=8] {'tm'}, use_global_device_ids=true, to_apply=%region_13.15 | all-reduce | flops 64 | bytes 512 | tf_op jit(solution)/shard_map/psum | solution.py:134
  153.6 80.1 %all-reduce.2 = (f32[256]{0:T(256)S(1)}, f32[256]{0:T(256)S(1)}) all-reduce(f32[256]{0:T(256)S(1)} %get-tuple-element.6, f32[256]{0:T(256)S(1)} %get-tuple-element.9), channel_id=1, replica_groups=mesh['dp'=16,'tm'=8] {'dp','tm'}, use_global_device_ids=true, to_apply=%region_16.18 | all-reduce | flops 512 | bytes 4096 | tf_op jit(solution)/shard_map/psum | solution.py:142
  233.6 3.9 fusion.33
  238.8 7.0 %pad_slice_fusion.24 = (bf16[8,16,16,256]{3,2,1,0:T(8,128)(2,1)}, bf16[8,16,16,256]{3,2,1,0:T(8,128)(2,1)S(1)}, bf16[8,16,16,256]{3,2,1,0:T(8,128)(2,1)}, bf16[8...) fusion(bf16[10,16,16,256]{3,2,1,0:T(8,128)(2,1)S(1)} %pad_maxim, ...), kind=kLoop, calls=%fused_computation.26 | loop fusion | bytes 21233664 | tf_op jit(solution)/shard_map/slice | solution.py:42
  245.8 2.7 pad_slice_fusion.25
  249.7 2.7 fusion.86
  258.4 1.2 fusion.23
  259.6 1.2 fusion.22
  269.1 1.2 fusion.15
  270.3 1.2 fusion.14
  279.9 1.2 fusion.6
  281.1 1.2 fusion.5
  284.8 2.2 convolution_add_fusion.51
  315.6 1.3 multiply_convert_fusion.1
  316.9 122.3 %all-reduce.6.cloned.1.call-done = f32[27,256,256]{2,1,0:T(8,128)} async-done(((f32[27,256,256]{2,1,0:T(8,128)}), f32[27,256,256]{2,1,0:T(8,128)}) %all-reduce.6.cloned.1.call-update) | async-done | bytes 7077904 | tf_op jit(solution)/shard_map/psum | solution.py:142
  439.2 6.8 %broadcast_multiply_fusion = f32[27,256,256]{2,1,0:T(8,128)} fusion(f32[27,256,256]{2,1,0:T(8,128)} %all-reduce.6.cloned.1.call-done), kind=kLoop, calls=%fused_computation.50 | loop fusion | flops 1769472 | bytes 14155776 | tf_op jit(solution)/shard_map/mul | solution.py:149
  (222 shorter events, 93.7 us)
Async XLA Ops:
  7.2 4.8 %copy-start = (bf16[1,8,16,16,256]{4,3,2,1,0:T(8,128)(2,1)S(1)}, bf16[1,8,16,16,256]{4,3,2,1,0:T(8,128)(2,1)}, u32[]{:S(2)}) copy-start(bf16[1,8,16,16,256]{4,3,2,1,0:T(8,128)(2,1)} %param.9) | copy-start | bytes 3145732
  7.2 432.0 %all-reduce.6.cloned.1.call-start = ((), (), s32[]{:S(2)}) async-start(), calls=%async_computation | async-start | bytes 14155776 | tf_op jit(solution)/shard_map/psum | solution.py:142
  11.9 3.1 copy-start.50
  12.0 3.7 copy-start.48
  12.0 6.5 %copy-start.4 = (bf16[1,8,16,16,256]{4,3,2,1,0:T(8,128)(2,1)S(1)}, bf16[1,8,16,16,256]{4,3,2,1,0:T(8,128)(2,1)}, u32[]{:S(2)}) copy-start(bf16[1,8,16,16,256]{4,3,2,1,0:T(8,128)(2,1)} %param.15) | copy-start | bytes 3145732
  13.7 70.5 %collective-permute-start = (bf16[8,16,16,256]{3,2,1,0:T(8,128)(2,1)}, bf16[8,16,16,256]{3,2,1,0:T(8,128)(2,1)}, u32[]{:S(2)}, u32[]{:S(2)}) collective-permute-start(bf16[8,16,16,256]{3,2,1,0:T(8,128)(2,1)} %select_multiply_fusion), channel_id=1, source_target_pairs={{1,0},{2,1},{3,2},{4,3},{5,4},{6,5},{7,6},{9,8},{10,9},{11,10},{12... | collective-permute-start | bytes 3145736 | tf_op jit(solution)/shard_map/ppermute | solution.py:17
  19.5 26.6 %collective-permute-start.2 = (bf16[2,16,16,256]{3,2,1,0:T(8,128)(2,1)}, bf16[2,16,16,256]{3,2,1,0:T(8,128)(2,1)S(1)}, u32[]{:S(2)}, u32[]{:S(2)}) collective-permute-start(bf16[2,16,16,256]{3,2,1,0:T(8,128)(2,1)} %slice.379), channel_id=1, source_target_pairs={{1,0},{2,1},{3,2},{4,3},{5,4},{6,5},{7,6},{9,8},{10,9},{11,10},{12... | collective-permute-start | bytes 786440 | tf_op jit(solution)/shard_map/ppermute | solution.py:17
  53.3 2.4 copy-start.2
  53.3 2.4 copy-start.10
  56.2 1.2 copy-start.46
  81.3 1.2 copy-start.29
  84.3 45.1 %copy-start.47 = (f32[256]{0:T(256)S(1)}, f32[256]{0:T(256)}, u32[]{:S(2)}) copy-start(f32[256]{0:T(256)} %param.13) | copy-start | bytes 3076
  84.3 45.1 %copy-start.49 = (f32[256]{0:T(256)S(1)}, f32[256]{0:T(256)}, u32[]{:S(2)}) copy-start(f32[256]{0:T(256)} %param.14) | copy-start | bytes 3076
  134.9 103.9 %collective-permute-start.1 = (bf16[2,16,16,256]{3,2,1,0:T(8,128)(2,1)}, bf16[2,16,16,256]{3,2,1,0:T(8,128)(2,1)S(1)}, u32[]{:S(2)}, u32[]{:S(2)}) collective-permute-start(bf16[2,16,16,256]{3,2,1,0:T(8,128)(2,1)} %slice.374), channel_id=1, source_target_pairs={{0,1},{1,2},{2,3},{3,4},{4,5},{5,6},{6,7},{8,9},{9,10},{10,11},{11... | collective-permute-start | bytes 786440 | tf_op jit(solution)/shard_map/ppermute | solution.py:17
  284.7 2.7 copy-start.3
  284.7 3.0 copy-start.28
  287.7 1.5 copy-start.27
  291.3 1.2 copy-start.25
  292.5 1.3 copy-start.24
  293.8 1.3 copy-start.23
  297.5 1.3 copy-start.20
  298.8 1.3 copy-start.19
  300.5 1.3 copy-start.18
  301.7 1.3 copy-start.17
  303.0 1.2 copy-start.16
  305.4 1.3 copy-start.14
  306.7 1.3 copy-start.13
  309.2 1.3 copy-start.7
  310.9 1.3 copy-start.6
  312.2 1.3 copy-start.5
  313.9 1.3 copy-start.11
  439.2 6.8 %copy-start.1 = (bf16[1,8,16,16,256]{4,3,2,1,0:T(8,128)(2,1)S(1)}, bf16[1,8,16,16,256]{4,3,2,1,0:T(8,128)(2,1)}, u32[]{:S(2)}) copy-start(bf16[1,8,16,16,256]{4,3,2,1,0:T(8,128)(2,1)} %param.9) | copy-start | bytes 3145732
  (23 other events, 28.2 us)
Sparse Core Ops, SparseCore 0:
  283.7 155.4 all-reduce.5
where the time goes:
time: 458 us; the launch traced here: 453 us
  waiting for transfers between devices  141 us (31%)
  blocking collectives  136 us (30%)
  matrix products  62.2 us (14%)
  local copies, waits for them, and re-layouts  58 us (13%)
  other arithmetic  33.6 us (7%)
  between operations  16.9 us (4%)
  starting transfers between devices  5.49 us (1%)
    psum x1, waiting for transfers between devices, body(): lax.psum((kernel_part, gain_part, bias_part), ('dp', 'tm'))  122 us
    psum x1, blocking collectives, body(): lax.psum((kernel_part, gain_part, bias_part), ('dp', 'tm'))  80.1 us
    unnamed x102, local copies, waits for them, and re-layouts  32.7 us
    dot_general x27, matrix products, tap_sweeps(): lax.dot_general(past_slice, grad_flat, (((0,), (0,)), ((), ())), preferre...  32.2 us
    psum x1, blocking collectives, body(): variance = lax.psum(group_total(centred * centred), 'tm') / cell_count  25.4 us
    ppermute x3, waiting for transfers between devices, shifted(): return lax.ppermute(block, axis, route)  18.9 us
    dot_general x27, matrix products, tap_sweeps(): jnp.dot(past_slice, weight[tap_index], preferred_element_type=jnp.float32)  16 us
    psum x1, blocking collectives, body(): group_means = lax.psum(group_total(inputs_f), 'tm') / cell_count  15.2 us
  transfers between devices with their start and end apart: 4, of which 2 were waited for; matrix products, arithmetic and copies ran while one was open for 12% of the time, Pallas kernels for 0%

commit v1 on v0

v1 whole, which is shorter than its diff:
```python
import functools
import math

import jax
import jax.numpy as jnp
from jax import lax
from jax.experimental import pallas as pl
from jax.experimental.pallas import tpu as pltpu
from jax.sharding import PartitionSpec as P

GROUPS = 32
EPSILON = 1e-05
MESH = pl.DeviceIdType.MESH
F32 = jnp.float32
BF16 = jnp.bfloat16

VMEM = pl.BlockSpec(memory_space=pltpu.VMEM)
SMEM = pl.BlockSpec(memory_space=pltpu.SMEM)


def params(limit, **others):
    return pltpu.CompilerParams(vmem_limit_bytes=limit << 20, **others)


def shifted(block, axis, distance):
    devices = range(lax.axis_size(axis))
    route = [(i - distance, i) for i in devices if i - distance in devices]
    return lax.ppermute(block, axis, route)


def start_of(len_ref, slabs, index):
    total = jnp.int32(0)
    for i in range(slabs):
        total = total + jnp.where(i < index, len_ref[0, i], 0)
    return total


def length_of(len_ref, slabs, index):
    total = jnp.int32(0)
    for i in range(slabs):
        total = total + jnp.where(i == index, len_ref[0, i], 0)
    return total


def group_sum(rows, width):
    lanes = rows.shape[1]
    lane = lax.broadcasted_iota(jnp.int32, rows.shape, 1)
    step = 1
    while step < width:
        up = pltpu.roll(rows, lanes - step, 1)
        down = pltpu.roll(rows, step, 1)
        rows = rows + jnp.where((lane & step) == 0, up, down)
        step *= 2
    return rows


def cells(res_ref, cols, shape):
    place = lax.broadcasted_iota(jnp.int32, shape, 0)
    return ((place // cols) < res_ref[0, 0]) & ((place % cols) < res_ref[0, 1])


def stats_kernel(slabs, cols, width, len_ref, res_ref, loaded_ref, stats_ref, tail_ref, mask_ref):
    frames, places, channels = loaded_ref.shape
    own = lax.axis_index("tm")
    length = length_of(len_ref, slabs, own)
    mask_ref[...] = cells(res_ref, cols, (places, channels)).astype(F32)
    count = (length * res_ref[0, 0] * res_ref[0, 1] * width).astype(F32)
    zero = jnp.zeros((8, channels), F32)

    def add_up(f, total):
        x = loaded_ref[f].astype(F32) * mask_ref[...]
        return total + jnp.sum(x.reshape(places // 8, 8, channels), axis=0)

    total = lax.fori_loop(0, length, add_up, zero)
    total = group_sum(jnp.broadcast_to(jnp.sum(total, axis=0, keepdims=True), (8, channels)), width)
    mean = total / count
    mean_row = mean[0:1]

    def spread(f, total):
        x = (loaded_ref[f].astype(F32) - mean_row) * mask_ref[...]
        return total + jnp.sum((x * x).reshape(places // 8, 8, channels), axis=0)

    squares = lax.fori_loop(0, length, spread, zero)
    squares = group_sum(
        jnp.broadcast_to(jnp.sum(squares, axis=0, keepdims=True), (8, channels)), width
    )
    row = lax.broadcasted_iota(jnp.int32, (8, channels), 0)
    stats_ref[...] = jnp.where(row == 0, mean, squares)
    first = own * frames + frames - 2 - start_of(len_ref, slabs, own)
    for k in range(2):
        offset = first + k
        usable = (offset >= 0) & (offset < length)
        picked = loaded_ref[jnp.clip(offset, 0, frames - 1)]
        tail_ref[k] = jnp.where(usable, picked, jnp.zeros_like(picked))


def share_kernel(size, mine_ref, all_ref, send_sem, recv_sem):
    own = lax.axis_index("tm")
    barrier = pltpu.get_barrier_semaphore()
    for off in range(1, size):
        peer = lax.rem(own + off, size)
        pl.semaphore_signal(barrier, inc=1, device_id={"tm": peer}, device_id_type=MESH)
    all_ref[own] = mine_ref[...]
    pl.semaphore_wait(barrier, size - 1)
    copies = []
    for off in range(1, size):
        peer = lax.rem(own + off, size)
        copy = pltpu.make_async_remote_copy(
            src_ref=mine_ref,
            dst_ref=all_ref.at[own],
            send_sem=send_sem.at[off],
            recv_sem=recv_sem.at[off],
            device_id={"tm": peer},
            device_id_type=MESH,
        )
        copy.start()
        copies.append(copy)
    for copy in copies:
        copy.wait()


def share(mine, size, collective_id):
    return pl.pallas_call(
        functools.partial(share_kernel, size),
        out_shape=jax.ShapeDtypeStruct((size,) + mine.shape, mine.dtype),
        in_specs=[VMEM],
        out_specs=VMEM,
        scratch_shapes=[pltpu.SemaphoreType.DMA((size,)), pltpu.SemaphoreType.DMA((size,))],
        compiler_params=pltpu.CompilerParams(collective_id=collective_id, has_side_effects=True),
    )(mine)


def lay_out(cat_ref, frame, value, rows, cols, first_col, last_col):
    places, channels = value.shape
    left = pltpu.roll(value, 1, 0) * first_col
    right = pltpu.roll(value, places - 1, 0) * last_col
    for k, part in enumerate((left, value, right)):
        cat_ref[frame, 1 : rows + 1, :, k * channels : (k + 1) * channels] = (
            part.astype(BF16).reshape(rows, cols, channels)
        )


def col_masks(cols, shape):
    place = lax.broadcasted_iota(jnp.int32, shape, 0) % cols
    return (place != 0).astype(F32), (place != cols - 1).astype(F32)


def back_kernel(
    slabs, rows, cols, len_ref, res_ref, cot_ref, next_ref, weight_ref, agrad_ref,
    cat_ref, turned_ref, mask_ref, first_ref, last_ref,
):
    frames, places, channels = cot_ref.shape
    own = lax.axis_index("tm")
    frame_total = start_of(len_ref, slabs, slabs)
    mask_ref[...] = cells(res_ref, cols, (places, channels)).astype(F32)
    first, last = col_masks(cols, (places, channels))
    first_ref[...] = first
    last_ref[...] = last

    def turn(block, _):
        for k in range(3):
            turned_ref[block, k * channels : (k + 1) * channels, :] = weight_ref[
                3 * block + 2 - k
            ].T
        return 0

    lax.fori_loop(0, 9, turn, 0)
    blank = jnp.zeros((cols, 3 * channels), BF16)

    def place(frame, value):
        alive = (own * frames + frame < frame_total).astype(F32)
        value = value.astype(F32) * (mask_ref[...] * alive)
        cat_ref[frame, 0] = blank
        cat_ref[frame, rows + 1] = blank
        lay_out(cat_ref, frame, value, rows, cols, first_ref[...], last_ref[...])

    def own_frame(f, _):
        place(f, cot_ref[f])
        return 0

    lax.fori_loop(0, frames, own_frame, 0)
    for k in range(2):
        place(frames + k, next_ref[k])

    def sweep(f, _):
        total = jnp.zeros((places, channels), F32)
        for d in range(3):
            for r in range(3):
                rows_in = cat_ref[f + 2 - d, 2 - r : 2 - r + rows].reshape(places, 3 * channels)
                total = total + jnp.dot(
                    rows_in, turned_ref[3 * d + r], preferred_element_type=F32
                )
        alive = (own * frames + f < frame_total).astype(F32)
        agrad_ref[f] = total * (mask_ref[...] * alive)
        return 0

    lax.fori_loop(0, frames, sweep, 0)


def main_kernel(
    slabs, rows, cols, width,
    len_ref, res_ref, loaded_ref, arrived_ref, tail_ref, cot_ref, agrad_ref, stats_ref,
    gain_ref, bias_ref, weight_ref,
    encoded_ref, kernel_ref, sums_ref, root_ref, ngrad_ref, normed_ref,
    cat_ref, grad_ref, mask_ref, first_ref, last_ref,
):
    frames, places, channels = cot_ref.shape
    own = lax.axis_index("tm")
    frame_total = start_of(len_ref, slabs, slabs)
    own_start, own_length = start_of(len_ref, slabs, own), length_of(len_ref, slabs, own)
    next_start, next_length = own_start + own_length, length_of(len_ref, slabs, own + 1)
    mask_ref[...] = cells(res_ref, cols, (places, channels)).astype(F32)
    first, last = col_masks(cols, (places, channels))
    first_ref[...] = first
    last_ref[...] = last

    area = res_ref[0, 0] * res_ref[0, 1] * width
    count = (frame_total * area).astype(F32)
    counts = [(len_ref[0, i] * area).astype(F32) for i in range(slabs)]
    mean = jnp.zeros((1, channels), F32)
    for i in range(slabs):
        mean = mean + counts[i] * stats_ref[i, 0:1]
    mean = mean / count
    squares = jnp.zeros((1, channels), F32)
    for i in range(slabs):
        apart = stats_ref[i, 0:1] - mean
        squares = squares + stats_ref[i, 1:2] + counts[i] * (apart * apart)
    root = lax.rsqrt(squares / count + EPSILON)
    root_ref[...] = jnp.broadcast_to(root, (8, channels))
    gain, bias = gain_ref[...], bias_ref[...]
    blank = jnp.zeros((cols, 3 * channels), BF16)

    def activate(slot, frame_id, value):
        alive = ((frame_id >= 0) & (frame_id < frame_total)).astype(F32)
        live = mask_ref[...] * alive
        normed = (value.astype(F32) * live - mean) * live * root
        pre = normed * gain + bias
        gate = 1.0 / (1.0 + jnp.exp(-pre))
        act = (pre * gate * live).astype(BF16).astype(F32)
        cat_ref[slot, 0] = blank
        cat_ref[slot, rows + 1] = blank
        lay_out(cat_ref, slot, act, rows, cols, first_ref[...], last_ref[...])
        return live, normed, pre, gate

    for k in range(2):
        frame_id = own * frames + k - 2
        offset = frame_id - own_start
        usable = (offset >= 0) & (offset < own_length)
        picked = jnp.where(usable, loaded_ref[jnp.clip(offset, 0, frames - 1)], tail_ref[k])
        activate(k, frame_id, picked)

    zero = jnp.zeros((8, channels), F32)

    def own_frame(f, sums):
        frame_id = own * frames + f
        offset = frame_id - own_start
        later = frame_id - next_start
        picked = jnp.where(
            offset < own_length,
            loaded_ref[jnp.clip(offset, 0, frames - 1)],
            arrived_ref[jnp.clip(later, 0, frames - 1)],
        )
        live, normed, pre, gate = activate(f + 2, frame_id, picked)
        grad_ref[pl.ds(pl.multiple_of(f * places, places), places)] = (
            cot_ref[f].astype(F32) * live
        ).astype(BF16)
        pre_grad = agrad_ref[f] * gate * (1.0 + pre * (1.0 - gate))
        normed_ref[f] = normed
        ngrad_ref[f] = pre_grad * gain
        return (
            sums[0] + jnp.sum((pre_grad * normed).reshape(places // 8, 8, channels), axis=0),
            sums[1] + jnp.sum(pre_grad.reshape(places // 8, 8, channels), axis=0),
        )

    gain_sum, bias_sum = lax.fori_loop(0, frames, own_frame, (zero, zero))
    row = lax.broadcasted_iota(jnp.int32, (8, channels), 0)
    sums_ref[...] = jnp.where(
        row == 0,
        jnp.sum(gain_sum, axis=0, keepdims=True),
        jnp.where(row == 1, jnp.sum(bias_sum, axis=0, keepdims=True), 0.0),
    )

    for d in range(3):
        for r in range(3):
            rows_in = cat_ref[d : d + frames, r : r + rows].reshape(frames * places, 3 * channels)
            kernel_ref[3 * d + r] = lax.dot_general(
                rows_in, grad_ref[...], (((0,), (0,)), ((), ())), preferred_element_type=F32
            ).astype(kernel_ref.dtype)

    def sweep(f, _):
        total = jnp.zeros((places, channels), F32)
        for d in range(3):
            for r in range(3):
                rows_in = cat_ref[f + d, r : r + rows].reshape(places, 3 * channels)
                total = total + jnp.dot(
                    rows_in, weight_ref[3 * d + r], preferred_element_type=F32
                )
        alive = (own * frames + f < frame_total).astype(F32)
        encoded_ref[f] = (total * (mask_ref[...] * alive)).astype(BF16)
        return 0

    lax.fori_loop(0, frames, sweep, 0)


def last_kernel(
    slabs, cols, width, frames,
    len_ref, res_ref, sums_ref, gain_ref, root_ref, ngrad_ref, normed_ref, out_ref,
):
    _, places, channels = ngrad_ref.shape
    own = lax.axis_index("tm")
    frame_total = start_of(len_ref, slabs, slabs)
    frame_id = own * frames + pl.program_id(0)
    count = (frame_total * res_ref[0, 0] * res_ref[0, 1] * width).astype(F32)
    total = sums_ref[0]
    for i in range(1, slabs):
        total = total + sums_ref[i]
    total = group_sum(total * gain_ref[...], width) / count
    live = (cells(res_ref, cols, (places, channels)) & (frame_id < frame_total)).astype(F32)
    inner = ngrad_ref[0] - total[1:2] - normed_ref[0] * total[0:1]
    out_ref[0] = (inner * root_ref[0:1] * live).astype(BF16)


def body(loaded, lengths, resolution, weight, norm_gain, norm_bias, cotangent):
    frames, rows, cols, channels = loaded.shape[1:]
    places, width = rows * cols, channels // GROUPS
    slabs = lax.axis_size("tm")
    shape = jax.ShapeDtypeStruct
    loaded = loaded.reshape(frames, places, channels)
    cotangent = cotangent.reshape(frames, places, channels)
    gain, bias = norm_gain.reshape(1, channels), norm_bias.reshape(1, channels)

    following = shifted(cotangent[:2], "tm", -1)
    arrived = shifted(loaded, "tm", -1)
    stats, tail = pl.pallas_call(
        functools.partial(stats_kernel, slabs, cols, width),
        out_shape=(shape((8, channels), F32), shape((2, places, channels), BF16)),
        in_specs=[SMEM, SMEM, VMEM],
        out_specs=(VMEM, VMEM),
        scratch_shapes=[pltpu.VMEM((places, channels), F32)],
        compiler_params=params(16),
        cost_estimate=pl.CostEstimate(flops=4 << 20, bytes_accessed=2 << 20, transcendentals=0),
    )(lengths, resolution, loaded)
    tail = shifted(tail, "tm", 1)
    all_stats = share(stats, slabs, 1)

    cat = pltpu.VMEM((frames + 2, rows + 2, cols, 3 * channels), BF16)
    plane = pltpu.VMEM((places, channels), F32)
    agrad = pl.pallas_call(
        functools.partial(back_kernel, slabs, rows, cols),
        out_shape=shape((frames, places, channels), F32),
        in_specs=[SMEM, SMEM, VMEM, VMEM, VMEM],
        out_specs=VMEM,
        scratch_shapes=[cat, pltpu.VMEM((9, 3 * channels, channels), BF16), plane, plane, plane],
        compiler_params=params(40),
        cost_estimate=pl.CostEstimate(
            flops=2 * 27 * frames * places * channels * channels,
            bytes_accessed=8 << 20,
            transcendentals=0,
        ),
    )(lengths, resolution, cotangent, following, weight)

    encoded, kernel_part, sums, root, ngrad, normed = pl.pallas_call(
        functools.partial(main_kernel, slabs, rows, cols, width),
        out_shape=(
            shape((frames, places, channels), BF16),
            shape((9, 3 * channels, channels), F32),
            shape((8, channels), F32),
            shape((8, channels), F32),
            shape((frames, places, channels), F32),
            shape((frames, places, channels), F32),
        ),
        in_specs=[SMEM, SMEM] + [VMEM] * 9,
        out_specs=(VMEM,) * 6,
        scratch_shapes=[cat, pltpu.VMEM((frames * places, channels), BF16), plane, plane, plane],
        compiler_params=params(56),
        cost_estimate=pl.CostEstimate(
            flops=4 * 27 * frames * places * channels * channels,
            bytes_accessed=20 << 20,
            transcendentals=frames * places * channels,
        ),
    )(
        lengths, resolution, loaded, arrived, tail, cotangent, agrad, all_stats,
        gain, bias, weight.reshape(9, 3 * channels, channels),
    )

    all_sums = share(sums, slabs, 2)
    block = pl.BlockSpec((1, places, channels), lambda f: (f, 0, 0))
    input_grad = pl.pallas_call(
        functools.partial(last_kernel, slabs, cols, width, frames),
        out_shape=shape((frames, places, channels), BF16),
        grid=(frames,),
        in_specs=[
            SMEM,
            SMEM,
            pl.BlockSpec((slabs, 8, channels), lambda f: (0, 0, 0)),
            pl.BlockSpec((1, channels), lambda f: (0, 0)),
            pl.BlockSpec((8, channels), lambda f: (0, 0)),
            block,
            block,
        ],
        out_specs=block,
        compiler_params=params(16),
    )(lengths, resolution, all_sums, gain, root, ngrad, normed)

    kernel_sum, pair_sum = lax.psum((kernel_part, sums[:2]), ("dp", "tm"))
    scale = 1.0 / math.sqrt(lax.axis_size("dp") * slabs * frames * places)
    whole = (1, frames, rows, cols, channels)
    return (
        encoded.reshape(whole),
        input_grad.reshape(whole),
        kernel_sum.reshape(27, channels, channels) * scale,
        pair_sum[0] * scale,
        pair_sum[1] * scale,
    )


def solution(mesh):
    slab = P("dp", "tm", None, None, None)
    return jax.shard_map(
        body,
        mesh=mesh,
        in_specs=(slab, P("dp", None), P("dp", None), P(), P(), P(), slab),
        out_specs=(slab, slab, P(), P(), P()),
        check_vma=False,
    )
```

time: 458 us -> 265 us (0.58); the launches traced: 453 us -> 265 us
  Pallas kernels: 0 us -> 74.5 us
  blocking collectives: 136 us -> 68.4 us
  waiting for transfers between devices: 141 us -> 77.9 us
  matrix products: 62.2 us -> 0 us
  local copies, waits for them, and re-layouts: 58 us -> 14.1 us
  other arithmetic: 33.6 us -> 7.16 us
    pallas_call x0 -> x6, Pallas kernels: none -> 74.5 us  [the longest x2 30.2 us: share(): pl.pallas_call(functools.partial(share_kernel, size), out_shape=jax.Shape...]
    psum x4 -> x1, blocking collectives: 136 us -> 68.4 us  [body(): kernel_sum, pair_sum = lax.psum((kernel_part, sums[:2]), ('dp', 'tm'))]
    dot_general x81 -> x0, matrix products: 62.2 us -> none  [the longest x27 32.2 us: tap_sweeps(): lax.dot_general(past_slice, grad_flat, (((0,), (0,)), ((), ())), preferre...]
    psum x1, waiting for transfers between devices: 122 us -> 77.9 us  [body(): kernel_sum, pair_sum = lax.psum((kernel_part, sums[:2]), ('dp', 'tm'))]
    unnamed x102 -> x36, local copies, waits for them, and re-layouts: 32.7 us -> 12.5 us
    slice x7 -> x2, local copies, waits for them, and re-layouts: 21.3 us -> 1.67 us  [the longest x1 0.97 us: body(): following = shifted(cotangent[:2], 'tm', -1)]
    ppermute x3, waiting for transfers between devices: 18.9 us -> 0.01 us  [shifted(): return lax.ppermute(block, axis, route)]
    reduce_sum x8 -> x0, other arithmetic: 9.63 us -> none  [the longest x1 4.71 us: body(): gain_part = jnp.sum(pre_grad * normed, axis=(0, 1, 2))]
  transfers between devices with their start and end apart: 4 -> 4, of which waited for: 2 -> 1; matrix products, arithmetic and copies ran while one was open for 12% -> 1% of each run, Pallas kernels for 0% -> 18%
where the time goes in v1:
time: 265 us
  waiting for transfers between devices  77.9 us (29%)
  Pallas kernels  74.5 us (28%)
  blocking collectives  68.4 us (26%)
  between operations  14.2 us (5%)
  local copies, waits for them, and re-layouts  14.1 us (5%)
  starting transfers between devices  8.54 us (3%)
  other arithmetic  7.16 us (3%)
    psum x1, waiting for transfers between devices, body(): kernel_sum, pair_sum = lax.psum((kernel_part, sums[:2]), ('dp', 'tm'))  77.9 us
    psum x1, blocking collectives, body(): kernel_sum, pair_sum = lax.psum((kernel_part, sums[:2]), ('dp', 'tm'))  68.4 us
    pallas_call x2, Pallas kernels, share(): pl.pallas_call(functools.partial(share_kernel, size), out_shape=jax.Shape...  30.2 us
    pallas_call x1, Pallas kernels, body(): pl.pallas_call(functools.partial(main_kernel, slabs, rows, cols, width),...  26.8 us
    unnamed x36, local copies, waits for them, and re-layouts  12.5 us
    pallas_call x1, Pallas kernels, body(): pl.pallas_call(functools.partial(back_kernel, slabs, rows, cols), out_sha...  11.6 us
    ppermute x3, starting transfers between devices, shifted(): return lax.ppermute(block, axis, route)  8.5 us
    mul x1, other arithmetic, body(): kernel_sum.reshape(27, channels, channels) * scale  6.59 us
  transfers between devices with their start and end apart: 4, of which 1 were waited for; matrix products, arithmetic and copies ran while one was open for 1% of the time, Pallas kernels for 18%

profile of v1, /device:TPU:1, one launch (start us, length us, event | category | flops | bytes accessed | tf_op | source)
XLA Modules:
  0.0 264.9 jit_solution(8914061147163988094)
XLA Ops:
  7.2 0.0 all-reduce.2.cloned.1.call-start
  7.2 1.3 collective-permute-start
  8.5 1.0 slice.15
  9.5 1.3 collective-permute-start.2
  10.8 0.0 copy-start.2
  10.8 1.2 copy-done.2
  12.0 0.7 copy-done.7
  12.7 0.7 copy-done.10
  13.3 1.1 shard_map.110
  14.4 0.6 copy-done.6
  15.0 5.9 %collective-permute-start.1 = (bf16[2,256,256]{2,1,0:T(8,128)(2,1)S(1)}, bf16[2,256,256]{2,1,0:T(8,128)(2,1)S(1)}, u32[]{:S(2)}, u32[]{:S(2)}) collective-permute-start(bf16[2,256,256]{2,1,0:T(8,128)(2,1)S(1)} %get-tuple-element.13), channel_id=1, source_target_pairs={{0,1},{1,2},{2,3},{3,4},{4,5},{5,6},{6,7},{8,9},{9,10},{10,11},{11... | collective-permute-start | bytes 786440 | tf_op jit(solution)/shard_map/ppermute | solution.py:28
  21.0 21.0 %shard_map.112.stats_ref = f32[8,8,256]{2,1,0:T(8,128)} custom-call(f32[8,256]{1,0:T(8,128)} %copy-done.6), custom_call_target="tpu_custom_call" | custom-call | tf_op jit(solution)/shard_map/pallas_call | solution.py:123
  42.0 0.0 copy-start.4
  42.0 1.2 copy-done.4
  43.2 0.7 copy-done.8
  43.9 0.7 copy-done.11
  44.5 2.0 copy-done.14
  46.5 11.6 %shard_map.111.agrad_ref = f32[8,256,256]{2,1,0:T(8,128)S(1)} custom-call(s32[1,8]{1,0:T(1,128)S(1)} %copy-done.8, s32[1,2]{1,0:T(1,128)S(1)} %copy-done.11, bf16[8,256,256]{2,1,0:T(8,128)(2,1)S(1)} %bitcast.15, bf16[2,256,256]{2,1,0:T(8,128)(2,1)S(1)} %collective-permute-done.2.next_ref, bf16[27,256,256]{2,1,0:T(8,128)(2,1)S(1)} %copy-done.14), custom_call_target="tpu_custom_call" | custom-call | flops 7247757312 | bytes 8388608 | tf_op jit(solution)/shard_map/pallas_call | solution.py:348
  58.2 1.3 copy-done.15
  59.5 0.7 copy-done.17
  60.2 0.4 copy-done.16
  60.6 26.8 %shard_map.113 = (bf16[8,256,256]{2,1,0:T(8,128)(2,1)}, f32[9,768,256]{2,1,0:T(8,128)}, f32[8,256]{1,0:T(8,128)}, f32[8,256]{1,0:T(8,128)}, f32[8,256,256]{2,1,0:T(8,128)}, /*index=5*/f32[8,256,256]{2,1,0:T(8,128)}) custom-call(s32[1,8]{1,0:T(1,128)} %len_ref.7, s32[1,2]{1,0:T(1,128)} %res_ref.7, bf16[8,256,256]{2,1,0:T(8,128)(2,1)} %bitcast.12, ...), custom_call_target="tpu_custom_call" | custom-call | flops 14495514624 | bytes 20971520 | tf_op jit(solution)/shard_map/pallas_call | solution.py:362
  87.5 0.0 all-reduce.2.cloned.1.call-update
  87.5 9.2 %shard_map.114.sums_ref = f32[8,8,256]{2,1,0:T(8,128)} custom-call(f32[8,256]{1,0:T(8,128)} %get-tuple-element.16.mine_ref), custom_call_target="tpu_custom_call" | custom-call | tf_op jit(solution)/shard_map/pallas_call | solution.py:123
  96.7 0.7 slice.17
  97.5 1.6 copy-done.1
  99.0 0.8 copy-done.3
  99.9 4.7 %shard_map.115 = bf16[8,256,256]{2,1,0:T(8,128)(2,1)} custom-call(s32[1,8]{1,0:T(1,128)S(1)} %copy-done.9, s32[1,2]{1,0:T(1,128)S(1)} %copy-done.12, f32[8,8,256]{2,1,0:T(8,128)S(1)} %copy-done.3, f32[1,256]{1,0:T(1,128)S(1)} %bitcast.17, f32[8,256]{1,0:T(8,128)S(1)} %copy-done.5, f32[8,256,256]{2,1,0:T(8,128)S(1)} %copy-done, f32[8,256,256]{2,1,0:T(8,128)S(1)} %copy-done.1), custom_call_target="tpu_custom_call" | custom-call | tf_op jit(solution)/shard_map/pallas_call | solution.py:388
  104.5 68.4 %psum.15 = f32[2,256]{1,0:T(2,128)S(1)} all-reduce(f32[2,256]{1,0:T(2,128)S(1)} %slice.17), channel_id=1, replica_groups=mesh['dp'=16,'tm'=8] {'dp','tm'}, use_global_device_ids=true, to_apply=%region_1.0 | all-reduce | flops 512 | bytes 4096 | tf_op jit(solution)/shard_map/psum | solution.py:405
  173.0 0.6 slice_multiply_fusion
  173.5 77.9 %all-reduce.2.cloned.1.call-done = f32[9,768,256]{2,1,0:T(8,128)} async-done(((f32[9,768,256]{2,1,0:T(8,128)}), f32[9,768,256]{2,1,0:T(8,128)}) %all-reduce.2.cloned.1.call-update) | async-done | bytes 7077904 | tf_op jit(solution)/shard_map/psum | solution.py:405
  251.4 6.6 %broadcast_multiply_fusion = f32[9,768,256]{2,1,0:T(8,128)} fusion(f32[9,768,256]{2,1,0:T(8,128)} %all-reduce.2.cloned.1.call-done), kind=kLoop, calls=%fused_computation | loop fusion | flops 1769472 | bytes 14155776 | tf_op jit(solution)/shard_map/mul | solution.py:411
  (24 shorter events, 0.1 us)
Async XLA Ops:
  7.2 244.3 %all-reduce.2.cloned.1.call-start = ((), (), s32[]{:S(2)}) async-start(), calls=%async_computation | async-start | bytes 14155776 | tf_op jit(solution)/shard_map/psum | solution.py:405
  7.2 52.3 %collective-permute-start = (bf16[8,256,256]{2,1,0:T(8,128)(2,1)}, bf16[8,256,256]{2,1,0:T(8,128)(2,1)S(1)}, u32[]{:S(2)}, u32[]{:S(2)}) collective-permute-start(bf16[8,256,256]{2,1,0:T(8,128)(2,1)} %bitcast.11), channel_id=1, source_target_pairs={{1,0},{2,1},{3,2},{4,3},{5,4},{6,5},{7,6},{9,8},{10,9},{11,10},{12... | collective-permute-start | bytes 3145736 | tf_op jit(solution)/shard_map/ppermute | solution.py:28
  9.5 32.5 %collective-permute-start.2 = (bf16[2,256,256]{2,1,0:T(8,128)(2,1)S(1)}, bf16[2,256,256]{2,1,0:T(8,128)(2,1)S(1)}, u32[]{:S(2)}, u32[]{:S(2)}) collective-permute-start(bf16[2,256,256]{2,1,0:T(8,128)(2,1)S(1)} %bitcast.21), channel_id=1, source_target_pairs={{1,0},{2,1},{3,2},{4,3},{5,4},{6,5},{7,6},{9,8},{10,9},{11,10},{12... | collective-permute-start | bytes 786440 | tf_op jit(solution)/shard_map/ppermute | solution.py:28
  10.8 1.2 copy-start.2
  12.0 0.7 copy-start.7
  12.7 0.7 copy-start.10
  14.4 0.6 copy-start.6
  15.0 44.5 %collective-permute-start.1 = (bf16[2,256,256]{2,1,0:T(8,128)(2,1)S(1)}, bf16[2,256,256]{2,1,0:T(8,128)(2,1)S(1)}, u32[]{:S(2)}, u32[]{:S(2)}) collective-permute-start(bf16[2,256,256]{2,1,0:T(8,128)(2,1)S(1)} %get-tuple-element.13), channel_id=1, source_target_pairs={{0,1},{1,2},{2,3},{3,4},{4,5},{5,6},{6,7},{8,9},{9,10},{10,11},{11... | collective-permute-start | bytes 786440 | tf_op jit(solution)/shard_map/ppermute | solution.py:28
  42.0 1.2 copy-start.4
  43.2 0.7 copy-start.8
  43.9 0.7 copy-start.11
  44.5 2.0 copy-start.14
  58.2 1.3 copy-start.15
  59.5 0.7 copy-start.17
  59.5 1.0 copy-start.16
  87.4 10.0 %copy-start = (f32[8,256,256]{2,1,0:T(8,128)S(1)}, f32[8,256,256]{2,1,0:T(8,128)}, u32[]{:S(2)}) copy-start(f32[8,256,256]{2,1,0:T(8,128)} %get-tuple-element.18.ngrad_ref) | copy-start | bytes 6291460
  87.4 10.0 %copy-start.5 = (f32[8,256]{1,0:T(8,128)S(1)}, f32[8,256]{1,0:T(8,128)}, u32[]{:S(2)}) copy-start(f32[8,256]{1,0:T(8,128)} %get-tuple-element.17.root_ref) | copy-start | bytes 24580
  87.4 10.0 %copy-start.9 = (s32[1,8]{1,0:T(1,128)S(1)}, s32[1,8]{1,0:T(1,128)}, u32[]{:S(2)}) copy-start(s32[1,8]{1,0:T(1,128)} %len_ref.7) | copy-start | bytes 100
  87.4 10.0 %copy-start.12 = (s32[1,2]{1,0:T(1,128)S(1)}, s32[1,2]{1,0:T(1,128)}, u32[]{:S(2)}) copy-start(s32[1,2]{1,0:T(1,128)} %res_ref.7) | copy-start | bytes 28
  87.5 10.0 %copy-start.13 = (f32[256]{0:T(256)S(1)}, f32[256]{0:T(256)}, u32[]{:S(2)}) copy-start(f32[256]{0:T(256)} %param.11) | copy-start | bytes 3076
  97.4 1.6 copy-start.1
  99.0 0.8 copy-start.3
Sparse Core Ops, SparseCore 0:
  87.6 163.7 all-reduce.1

commit v2 on v1

--- a/solution.py
+++ b/solution.py
@@ -320,6 +320,243 @@
     out_ref[0] = (inner * root_ref[0:1] * live).astype(BF16)
 
 
+def reduce_kernel(
+    blocks, mine_ref, sums_ref, total_ref, slabs_ref, pair_ref,
+    core_in, send1, in1, send2, in2, in3, tm_total, core_sum, x_sums, x_total, z_sum,
+    send_sem, recv_sem, pair_send, pair_recv,
+):
+    dp, tm = lax.axis_index("dp"), lax.axis_index("tm")
+    core, x, y = dp % 2, dp // 4, tm % 4
+    z = (dp // 2) % 2 * 2 + tm // 4
+    here = (x, y, z)
+    part, piece = blocks // 4, blocks // 16
+
+    def device(place, its_core):
+        return ((place[0] * 2 + place[2] // 2) * 2 + its_core, (place[2] % 2) * 4 + place[1])
+
+    def along(axis, off):
+        place = list(here)
+        place[axis] = (here[axis] + off) % 4
+        return place[axis], device(place, core)
+
+    other = device(here, 1 - core)
+    across = device((x, y, (z + 2) % 4), core)
+    tm_peers = [(dp, (tm + off) % 8) for off in range(1, 8)]
+    axis_peers = [along(axis, off)[1] for axis in (0, 1, 2) for off in (1, 2, 3)]
+    barrier = pltpu.get_barrier_semaphore()
+    greeted = [other] + axis_peers + tm_peers
+    for peer in greeted:
+        pl.semaphore_signal(barrier, inc=1, device_id=peer, device_id_type=MESH)
+    pl.semaphore_wait(barrier, len(greeted))
+
+    def send(src, dst, sems, peer):
+        copy = pltpu.make_async_remote_copy(
+            src_ref=src, dst_ref=dst, send_sem=sems[0], recv_sem=sems[1],
+            device_id=peer, device_id_type=MESH,
+        )
+        copy.start()
+        return copy
+
+    def sems(stage, stream, peer):
+        return send_sem.at[stage, stream, peer], recv_sem.at[stage, stream, peer]
+
+    def pair_sems(i):
+        return pair_send.at[i], pair_recv.at[i]
+
+    lanes = mine_ref.shape[-1] // 2
+    own_lanes = pl.ds(pl.multiple_of(core * lanes, lanes), lanes)
+    far_lanes = pl.ds(pl.multiple_of((1 - core) * lanes, lanes), lanes)
+    order = [(k % 3, (k + 1) % 3, (k + 2) % 3) for k in range(3)]
+
+    started = []
+    halves = []
+    for k in range(3):
+        halves.append(
+            send(mine_ref.at[k, :, :, far_lanes], core_in.at[k], sems(0, k, 0), other)
+        )
+    slabs_ref[tm] = sums_ref[...]
+    shares = [
+        send(sums_ref, slabs_ref.at[tm], pair_sems(i), peer) for i, peer in enumerate(tm_peers)
+    ]
+
+    firsts = []
+    for k in range(3):
+        halves[k].wait()
+
+        def add_half(b, _, k=k):
+            at = pl.ds(b * 4, 4)
+            both = mine_ref[k, at]
+            own = jnp.where(core == 0, both[..., :lanes], both[..., lanes:])
+            send1[k, at] = (own.astype(F32) + core_in[k, at].astype(F32)).astype(BF16)
+            return 0
+
+        lax.fori_loop(0, blocks // 4, add_half, 0)
+        axis = order[k][0]
+        row = []
+        for off in (1, 2, 3):
+            there, peer = along(axis, off)
+            row.append(
+                send(
+                    send1.at[k, pl.ds(there * part, part)],
+                    in1.at[k, off - 1],
+                    sems(1, k, off - 1),
+                    peer,
+                )
+            )
+        firsts.append(row)
+
+    for copy in shares:
+        copy.wait()
+    total = slabs_ref[0]
+    for i in range(1, 8):
+        total = total + slabs_ref[i]
+    tm_total[...] = total
+    core_copy = send(tm_total, core_sum, pair_sems(7), other)
+    core_copy.wait()
+    x_sums[x] = tm_total[...] + core_sum[...]
+    x_copies = []
+    for off in (1, 2, 3):
+        _, peer = along(0, off)
+        x_copies.append(send(x_sums.at[x], x_sums.at[x], pair_sems(7 + off), peer))
+
+    seconds = []
+    for k in range(3):
+        for copy in firsts[k]:
+            copy.wait()
+        base = here[order[k][0]] * part
+
+        def add_first(b, _, k=k, base=base):
+            at = pl.ds(b * 3, 3)
+            own = send1[k, pl.ds(base + b * 3, 3)].astype(F32)
+            for i in range(3):
+                own = own + in1[k, i, at].astype(F32)
+            send2[k, at] = own.astype(BF16)
+            return 0
+
+        lax.fori_loop(0, part // 3, add_first, 0)
+        axis = order[k][1]
+        row = []
+        for off in (1, 2, 3):
+            there, peer = along(axis, off)
+            row.append(
+                send(
+                    send2.at[k, pl.ds(there * piece, piece)],
+                    in2.at[k, off - 1],
+                    sems(2, k, off - 1),
+                    peer,
+                )
+            )
+        seconds.append(row)
+
+    for copy in x_copies:
+        copy.wait()
+    x_total[...] = x_sums[0] + x_sums[1] + x_sums[2] + x_sums[3]
+    z_copy = send(x_total, z_sum, pair_sems(11), across)
+
+    thirds = []
+    for k in range(3):
+        for copy in seconds[k]:
+            copy.wait()
+        base = here[order[k][1]] * piece
+        spot = here[order[k][2]]
+
+        def add_second(b, _, k=k, base=base, spot=spot):
+            at = pl.ds(b * 3, 3)
+            own = send2[k, pl.ds(base + b * 3, 3)].astype(F32)
+            for i in range(3):
+                own = own + in2[k, i, at].astype(F32)
+            in3[k, spot, at] = own.astype(BF16)
+            return 0
+
+        lax.fori_loop(0, piece // 3, add_second, 0)
+        axis = order[k][2]
+        row = []
+        for off in (1, 2, 3):
+            _, peer = along(axis, off)
+            row.append(send(in3.at[k, spot], in3.at[k, spot], sems(3, k, off - 1), peer))
+        thirds.append(row)
+
+    z_copy.wait()
+    pair_ref[...] = x_total[...] + z_sum[...]
+
+    fourths = []
+    for k in range(3):
+        for copy in thirds[k]:
+            copy.wait()
+        base = here[order[k][0]] * part + here[order[k][1]] * piece
+
+        def add_third(b, _, k=k, base=base):
+            at = pl.ds(b * 3, 3)
+            own = in3[k, 0, at].astype(F32)
+            for i in range(1, 4):
+                own = own + in3[k, i, at].astype(F32)
+            total_ref[k, pl.ds(base + b * 3, 3), :, own_lanes] = own.astype(BF16)
+            return 0
+
+        lax.fori_loop(0, piece // 3, add_third, 0)
+        spot = total_ref.at[k, pl.ds(base, piece), :, own_lanes]
+        row = []
+        for off in (1, 2, 3):
+            _, peer = along(order[k][1], off)
+            row.append(send(spot, spot, sems(4, k, off - 1), peer))
+        fourths.append(row)
+    fifths = []
+    for k in range(3):
+        for copy in fourths[k]:
+            copy.wait()
+        spot = total_ref.at[k, pl.ds(here[order[k][0]] * part, part), :, own_lanes]
+        row = []
+        for off in (1, 2, 3):
+            _, peer = along(order[k][0], off)
+            row.append(send(spot, spot, sems(5, k, off - 1), peer))
+        fifths.append(row)
+    for k in range(3):
+        for copy in fifths[k]:
+            copy.wait()
+        spot = total_ref.at[k, :, :, own_lanes]
+        started.append(send(spot, spot, sems(6, k, 0), other))
+    for copy in started:
+        copy.wait()
+
+
+def reduce_all(mine, sums, slabs, collective_id):
+    streams, blocks, sub, channels = mine.shape
+    part, piece, lanes = blocks // 4, blocks // 16, channels // 2
+    small = pltpu.VMEM(sums.shape, F32)
+
+    def slots(*lead):
+        return pltpu.VMEM(lead + (sub, lanes), BF16)
+
+    return pl.pallas_call(
+        functools.partial(reduce_kernel, blocks),
+        out_shape=(
+            jax.ShapeDtypeStruct(mine.shape, BF16),
+            jax.ShapeDtypeStruct((slabs,) + sums.shape, F32),
+            jax.ShapeDtypeStruct(sums.shape, F32),
+        ),
+        in_specs=[VMEM, VMEM],
+        out_specs=(VMEM,) * 3,
+        scratch_shapes=[
+            slots(streams, blocks),
+            slots(streams, blocks),
+            slots(streams, 3, part),
+            slots(streams, part),
+            slots(streams, 3, piece),
+            slots(streams, 4, piece),
+            small,
+            small,
+            pltpu.VMEM((4,) + sums.shape, F32),
+            small,
+            small,
+            pltpu.SemaphoreType.DMA((7, streams, 3)),
+            pltpu.SemaphoreType.DMA((7, streams, 3)),
+            pltpu.SemaphoreType.DMA((12,)),
+            pltpu.SemaphoreType.DMA((12,)),
+        ],
+        compiler_params=params(40, collective_id=collective_id, has_side_effects=True),
+    )(mine, sums)
+
+
 def body(loaded, lengths, resolution, weight, norm_gain, norm_bias, cotangent):
     frames, rows, cols, channels = loaded.shape[1:]
     places, width = rows * cols, channels // GROUPS
@@ -341,8 +578,6 @@
         cost_estimate=pl.CostEstimate(flops=4 << 20, bytes_accessed=2 << 20, transcendentals=0),
     )(lengths, resolution, loaded)
     tail = shifted(tail, "tm", 1)
-    all_stats = share(stats, slabs, 1)
-
     cat = pltpu.VMEM((frames + 2, rows + 2, cols, 3 * channels), BF16)
     plane = pltpu.VMEM((places, channels), F32)
     agrad = pl.pallas_call(
@@ -358,12 +593,14 @@
             transcendentals=0,
         ),
     )(lengths, resolution, cotangent, following, weight)
+    stats, agrad = lax.optimization_barrier((stats, agrad))
+    all_stats = share(stats, slabs, 1)
 
     encoded, kernel_part, sums, root, ngrad, normed = pl.pallas_call(
         functools.partial(main_kernel, slabs, rows, cols, width),
         out_shape=(
             shape((frames, places, channels), BF16),
-            shape((9, 3 * channels, channels), F32),
+            shape((9, 3 * channels, channels), BF16),
             shape((8, channels), F32),
             shape((8, channels), F32),
             shape((frames, places, channels), F32),
@@ -383,7 +620,9 @@
         gain, bias, weight.reshape(9, 3 * channels, channels),
     )
 
-    all_sums = share(sums, slabs, 2)
+    total, all_sums, pair = reduce_all(
+        kernel_part.reshape(3, 9 * channels // 16, 16, channels), sums, slabs, 2
+    )
     block = pl.BlockSpec((1, places, channels), lambda f: (f, 0, 0))
     input_grad = pl.pallas_call(
         functools.partial(last_kernel, slabs, cols, width, frames),
@@ -402,15 +641,14 @@
         compiler_params=params(16),
     )(lengths, resolution, all_sums, gain, root, ngrad, normed)
 
-    kernel_sum, pair_sum = lax.psum((kernel_part, sums[:2]), ("dp", "tm"))
     scale = 1.0 / math.sqrt(lax.axis_size("dp") * slabs * frames * places)
     whole = (1, frames, rows, cols, channels)
     return (
         encoded.reshape(whole),
         input_grad.reshape(whole),
-        kernel_sum.reshape(27, channels, channels) * scale,
-        pair_sum[0] * scale,
-        pair_sum[1] * scale,
+        total.reshape(27, channels, channels).astype(F32) * scale,
+        pair[0] * scale,
+        pair[1] * scale,
     )
 
 

time: 265 us -> 144 us (0.54)
  blocking collectives: 68.4 us -> 0 us
  waiting for transfers between devices: 77.9 us -> 18.5 us
  Pallas kernels: 74.5 us -> 98 us
  between operations: 14.2 us -> 0.79 us
    psum x1 -> x0, waiting for transfers between devices: 77.9 us -> none  [body(): kernel_sum, pair_sum = lax.psum((kernel_part, sums[:2]), ('dp', 'tm'))]
    psum x1 -> x0, blocking collectives: 68.4 us -> none  [body(): kernel_sum, pair_sum = lax.psum((kernel_part, sums[:2]), ('dp', 'tm'))]
    pallas_call x0 -> x1, Pallas kernels: none -> 44.6 us  [reduce_all(): pl.pallas_call(functools.partial(reduce_kernel, blocks), out_shape=(jax.S...]
    pallas_call x2 -> x1, Pallas kernels: 30.2 us -> 9.77 us  [share(): pl.pallas_call(functools.partial(share_kernel, size), out_shape=jax.Shape...]
    ppermute x3, waiting for transfers between devices: 0.01 us -> 18.5 us  [shifted(): return lax.ppermute(block, axis, route)]
    unnamed x36 -> x38, local copies, waits for them, and re-layouts: 12.5 us -> 12.7 us
  transfers between devices with their start and end apart: 4 -> 3, of which waited for: 1 -> 1; matrix products, arithmetic and copies ran while one was open for 1% -> 1% of each run, Pallas kernels for 18% -> 16%
where the time goes in v2:
time: 144 us
  Pallas kernels  98 us (68%)
  waiting for transfers between devices  18.5 us (13%)
  local copies, waits for them, and re-layouts  13.7 us (10%)
  starting transfers between devices  8.27 us (6%)
  other arithmetic  4.55 us (3%)
    pallas_call x1, Pallas kernels, reduce_all(): pl.pallas_call(functools.partial(reduce_kernel, blocks), out_shape=(jax.S...  44.6 us
    pallas_call x1, Pallas kernels, body(): pl.pallas_call(functools.partial(main_kernel, slabs, rows, cols, width),...  25.8 us
    ppermute x3, waiting for transfers between devices, shifted(): return lax.ppermute(block, axis, route)  18.5 us
    unnamed x38, local copies, waits for them, and re-layouts  12.7 us
    pallas_call x1, Pallas kernels, body(): pl.pallas_call(functools.partial(back_kernel, slabs, rows, cols), out_sha...  11.7 us
    pallas_call x1, Pallas kernels, share(): pl.pallas_call(functools.partial(share_kernel, size), out_shape=jax.Shape...  9.77 us
    ppermute x3, starting transfers between devices, shifted(): return lax.ppermute(block, axis, route)  8.27 us
    pallas_call x1, Pallas kernels, body(): pl.pallas_call(functools.partial(last_kernel, slabs, cols, width, frames)...  4.7 us
  transfers between devices with their start and end apart: 3, of which 1 were waited for; matrix products, arithmetic and copies ran while one was open for 1% of the time, Pallas kernels for 16%

profile of v2, /device:TPU:1, one launch (start us, length us, event | category | flops | bytes accessed | tf_op | source)
XLA Modules:
  0.0 143.8 jit_solution(12147644098063660028)
XLA Ops:
  0.6 1.3 collective-permute-start
  1.9 1.0 slice.12
  2.9 1.3 collective-permute-start.2
  4.2 0.0 copy-start.3
  4.2 1.2 copy-done.3
  5.4 0.7 copy-done.8
  6.1 0.7 copy-done.11
  6.7 1.4 shard_map.110
  8.2 0.6 copy-done.7
  8.8 5.7 %collective-permute-start.1 = (bf16[2,256,256]{2,1,0:T(8,128)(2,1)S(1)}, bf16[2,256,256]{2,1,0:T(8,128)(2,1)S(1)}, u32[]{:S(2)}, u32[]{:S(2)}) collective-permute-start(bf16[2,256,256]{2,1,0:T(8,128)(2,1)S(1)} %get-tuple-element.18), channel_id=1, source_target_pairs={{0,1},{1,2},{2,3},{3,4},{4,5},{5,6},{6,7},{8,9},{9,10},{10,11},{11... | collective-permute-start | bytes 786440 | tf_op jit(solution)/shard_map/ppermute | solution.py:28
  14.5 18.5 %collective-permute-done.2.next_ref = bf16[2,256,256]{2,1,0:T(8,128)(2,1)S(1)} collective-permute-done((bf16[2,256,256]{2,1,0:T(8,128)(2,1)S(1)}, bf16[2,256,256]{2,1,0:T(8,128)(2,1)S(1)}, u32[]{:S(2)}, u32[]{:S(2)}) %collective-permute-start.2) | collective-permute-done | bytes 262176 | tf_op jit(solution)/shard_map/ppermute | solution.py:28
  33.0 1.2 copy-done.4
  34.2 0.7 copy-done.9
  34.9 0.7 copy-done.12
  35.5 2.0 %copy-done.15 = bf16[27,256,256]{2,1,0:T(8,128)(2,1)S(1)} copy-done((bf16[27,256,256]{2,1,0:T(8,128)(2,1)S(1)}, bf16[27,256,256]{2,1,0:T(8,128)(2,1)}, u32[]{:S(2)}) %copy-start.15) | copy-done | bytes 3538968
  37.5 11.7 %shard_map.111.agrad_ref = f32[8,256,256]{2,1,0:T(8,128)S(1)} custom-call(s32[1,8]{1,0:T(1,128)S(1)} %copy-done.9, s32[1,2]{1,0:T(1,128)S(1)} %copy-done.12, bf16[8,256,256]{2,1,0:T(8,128)(2,1)S(1)} %bitcast.17, bf16[2,256,256]{2,1,0:T(8,128)(2,1)S(1)} %collective-permute-done.2.next_ref, bf16[27,256,256]{2,1,0:T(8,128)(2,1)S(1)} %copy-done.15), custom_call_target="tpu_custom_call" | custom-call | flops 7247757312 | bytes 8388608 | tf_op jit(solution)/shard_map/pallas_call | solution.py:583
  49.2 1.3 copy-done.16
  50.5 9.8 %shard_map.112.stats_ref = f32[8,8,256]{2,1,0:T(8,128)} custom-call(f32[8,256]{1,0:T(8,128)} %copy-done.7), custom_call_target="tpu_custom_call" | custom-call | tf_op jit(solution)/shard_map/pallas_call | solution.py:123
  60.3 0.0 collective-permute-done.1.tail_ref
  60.3 0.0 collective-permute-done.arrived_ref
  60.3 0.0 copy-start.17
  60.3 0.7 copy-done.18
  61.0 0.3 copy-done.17
  61.4 25.8 %shard_map.113 = (bf16[8,256,256]{2,1,0:T(8,128)(2,1)}, bf16[9,768,256]{2,1,0:T(8,128)(2,1)}, f32[8,256]{1,0:T(8,128)}, f32[8,256]{1,0:T(8,128)}, f32[8,256,256]{2,1,0:T(8,128)}, /*index=5*/f32[8,256,256]{2,1,0:T(8,128)}) custom-call(s32[1,8]{1,0:T(1,128)} %len_ref.7, s32[1,2]{1,0:T(1,128)} %res_ref.7, bf16[8,256,256]{2,1,0:T(8,128)(2,1)} %bitcast.14, ...), custom_call_target="tpu_custom_call" | custom-call | flops 14495514624 | bytes 20971520 | tf_op jit(solution)/shard_map/pallas_call | solution.py:599
  87.2 2.0 %copy-done = bf16[9,768,256]{2,1,0:T(8,128)(2,1)S(1)} copy-done((bf16[9,768,256]{2,1,0:T(8,128)(2,1)S(1)}, bf16[9,768,256]{2,1,0:T(8,128)(2,1)}, u32[]{:S(2)}) %copy-start) | copy-done | bytes 3538968
  89.2 0.7 copy-done.6
  89.9 44.6 %shard_map.114 = (bf16[3,144,16,256]{3,2,1,0:T(8,128)(2,1)S(1)}, f32[8,8,256]{2,1,0:T(8,128)S(1)}, f32[8,256]{1,0:T(8,128)S(1)}) custom-call(bf16[3,144,16,256]{3,2,1,0:T(8,128)(2,1)S(1)} %bitcast.12, f32[8,256]{1,0:T(8,128)S(1)} %copy-done.6), custom_call_target="tpu_custom_call" | custom-call | tf_op jit(solution)/shard_map/pallas_call | solution.py:530
  134.5 0.6 slice_multiply_fusion
  135.1 0.0 copy-start.13
  135.1 0.0 copy-start.14
  135.1 4.0 %convert_multiply_fusion = f32[3,144,16,256]{3,2,1,0:T(8,128)} fusion(bf16[3,144,16,256]{3,2,1,0:T(8,128)(2,1)S(1)} %get-tuple-element.29), kind=kLoop, calls=%fused_computation | loop fusion | flops 3538944 | bytes 10616832 | tf_op jit(solution)/shard_map/mul | solution.py:649
  139.1 4.7 %shard_map.115 = bf16[8,256,256]{2,1,0:T(8,128)(2,1)} custom-call(s32[1,8]{1,0:T(1,128)S(1)} %copy-done.10, s32[1,2]{1,0:T(1,128)S(1)} %copy-done.13, f32[8,8,256]{2,1,0:T(8,128)S(1)} %get-tuple-element.25.sums_ref, f32[1,256]{1,0:T(1,128)S(1)} %bitcast.19, f32[8,256]{1,0:T(8,128)S(1)} %copy-done.5, f32[8,256,256]{2,1,0:T(8,128)S(1)} %copy-done.1, ...), custom_call_target="tpu_custom_call" | custom-call | tf_op jit(solution)/shard_map/pallas_call | solution.py:627
  (21 shorter events, 0.0 us)
Async XLA Ops:
  0.6 59.7 %collective-permute-start = (bf16[8,256,256]{2,1,0:T(8,128)(2,1)}, bf16[8,256,256]{2,1,0:T(8,128)(2,1)S(1)}, u32[]{:S(2)}, u32[]{:S(2)}) collective-permute-start(bf16[8,256,256]{2,1,0:T(8,128)(2,1)} %bitcast.13), channel_id=1, source_target_pairs={{1,0},{2,1},{3,2},{4,3},{5,4},{6,5},{7,6},{9,8},{10,9},{11,10},{12... | collective-permute-start | bytes 3145736 | tf_op jit(solution)/shard_map/ppermute | solution.py:28
  2.9 30.1 %collective-permute-start.2 = (bf16[2,256,256]{2,1,0:T(8,128)(2,1)S(1)}, bf16[2,256,256]{2,1,0:T(8,128)(2,1)S(1)}, u32[]{:S(2)}, u32[]{:S(2)}) collective-permute-start(bf16[2,256,256]{2,1,0:T(8,128)(2,1)S(1)} %bitcast.23), channel_id=1, source_target_pairs={{1,0},{2,1},{3,2},{4,3},{5,4},{6,5},{7,6},{9,8},{10,9},{11,10},{12... | collective-permute-start | bytes 786440 | tf_op jit(solution)/shard_map/ppermute | solution.py:28
  4.2 1.2 copy-start.3
  5.4 0.7 copy-start.8
  6.1 0.7 copy-start.11
  8.2 0.6 copy-start.7
  8.8 51.5 %collective-permute-start.1 = (bf16[2,256,256]{2,1,0:T(8,128)(2,1)S(1)}, bf16[2,256,256]{2,1,0:T(8,128)(2,1)S(1)}, u32[]{:S(2)}, u32[]{:S(2)}) collective-permute-start(bf16[2,256,256]{2,1,0:T(8,128)(2,1)S(1)} %get-tuple-element.18), channel_id=1, source_target_pairs={{0,1},{1,2},{2,3},{3,4},{4,5},{5,6},{6,7},{8,9},{9,10},{10,11},{11... | collective-permute-start | bytes 786440 | tf_op jit(solution)/shard_map/ppermute | solution.py:28
  33.0 1.2 copy-start.4
  34.2 0.7 copy-start.9
  34.8 0.7 copy-start.12
  35.5 2.0 %copy-start.15 = (bf16[27,256,256]{2,1,0:T(8,128)(2,1)S(1)}, bf16[27,256,256]{2,1,0:T(8,128)(2,1)}, u32[]{:S(2)}) copy-start(bf16[27,256,256]{2,1,0:T(8,128)(2,1)} %weight_ref.1) | copy-start | bytes 10616836
  49.2 1.3 copy-start.16
  60.3 0.7 copy-start.18
  60.3 1.0 copy-start.17
  87.2 2.0 %copy-start = (bf16[9,768,256]{2,1,0:T(8,128)(2,1)S(1)}, bf16[9,768,256]{2,1,0:T(8,128)(2,1)}, u32[]{:S(2)}) copy-start(bf16[9,768,256]{2,1,0:T(8,128)(2,1)} %get-tuple-element.23) | copy-start | bytes 10616836
  89.2 0.7 copy-start.6
  135.1 4.0 %copy-start.1 = (f32[8,256,256]{2,1,0:T(8,128)S(1)}, f32[8,256,256]{2,1,0:T(8,128)}, u32[]{:S(2)}) copy-start(f32[8,256,256]{2,1,0:T(8,128)} %get-tuple-element.27.ngrad_ref) | copy-start | bytes 6291460
  135.1 4.0 %copy-start.2 = (f32[8,256,256]{2,1,0:T(8,128)S(1)}, f32[8,256,256]{2,1,0:T(8,128)}, u32[]{:S(2)}) copy-start(f32[8,256,256]{2,1,0:T(8,128)} %get-tuple-element.28.normed_ref) | copy-start | bytes 6291460
  135.1 4.0 %copy-start.5 = (f32[8,256]{1,0:T(8,128)S(1)}, f32[8,256]{1,0:T(8,128)}, u32[]{:S(2)}) copy-start(f32[8,256]{1,0:T(8,128)} %get-tuple-element.26.root_ref) | copy-start | bytes 24580
  135.1 4.0 %copy-start.10 = (s32[1,8]{1,0:T(1,128)S(1)}, s32[1,8]{1,0:T(1,128)}, u32[]{:S(2)}) copy-start(s32[1,8]{1,0:T(1,128)} %len_ref.7) | copy-start | bytes 100
  135.1 4.0 %copy-start.13 = (s32[1,2]{1,0:T(1,128)S(1)}, s32[1,2]{1,0:T(1,128)}, u32[]{:S(2)}) copy-start(s32[1,2]{1,0:T(1,128)} %res_ref.7) | copy-start | bytes 28
  135.1 4.0 %copy-start.14 = (f32[256]{0:T(256)S(1)}, f32[256]{0:T(256)}, u32[]{:S(2)}) copy-start(f32[256]{0:T(256)} %param.11) | copy-start | bytes 3076

commit v3 on v1

v3 whole, which is shorter than its diff:
```python
import functools
import math

import jax
import jax.numpy as jnp
from jax import lax
from jax.experimental import pallas as pl
from jax.experimental.pallas import tpu as pltpu
from jax.sharding import PartitionSpec as P

GROUPS = 32
EPSILON = 1e-05
MESH = pl.DeviceIdType.MESH
F32 = jnp.float32
BF16 = jnp.bfloat16

VMEM = pl.BlockSpec(memory_space=pltpu.VMEM)
ANY = pl.BlockSpec(memory_space=pl.ANY)
SMEM = pl.BlockSpec(memory_space=pltpu.SMEM)


def params(limit, **others):
    return pltpu.CompilerParams(vmem_limit_bytes=limit << 20, **others)


def start_of(len_ref, slabs, index):
    total = jnp.int32(0)
    for i in range(slabs):
        total = total + jnp.where(i < index, len_ref[0, i], 0)
    return total


def length_of(len_ref, slabs, index):
    total = jnp.int32(0)
    for i in range(slabs):
        total = total + jnp.where(i == index, len_ref[0, i], 0)
    return total


def group_sum(rows, width):
    lanes = rows.shape[1]
    lane = lax.broadcasted_iota(jnp.int32, rows.shape, 1)
    step = 1
    while step < width:
        up = pltpu.roll(rows, lanes - step, 1)
        down = pltpu.roll(rows, step, 1)
        rows = rows + jnp.where((lane & step) == 0, up, down)
        step *= 2
    return rows


def cells(res_ref, cols, shape):
    place = lax.broadcasted_iota(jnp.int32, shape, 0)
    return ((place // cols) < res_ref[0, 0]) & ((place % cols) < res_ref[0, 1])


def lay_out(cat_ref, frame, value, rows, cols, first_col, last_col):
    places, channels = value.shape
    left = pltpu.roll(value, 1, 0) * first_col
    right = pltpu.roll(value, places - 1, 0) * last_col
    for k, part in enumerate((left, value, right)):
        cat_ref[frame, 1 : rows + 1, :, k * channels : (k + 1) * channels] = (
            part.astype(BF16).reshape(rows, cols, channels)
        )


def col_masks(cols, shape):
    place = lax.broadcasted_iota(jnp.int32, shape, 0) % cols
    return (place != 0).astype(F32), (place != cols - 1).astype(F32)


def section_kernel(
    rows, cols, width,
    len_ref, res_ref, loaded_hbm, cot_hbm, weight_hbm, gain_ref, bias_ref,
    encoded_hbm, igrad_hbm, total_ref, pair_ref,
    loaded_ref, arrived_ref, cot_ref, next_ref, tail_out, tail_ref, weight_ref, turned_ref,
    back_cat, cat_ref, grad_ref, agrad_ref, normed_ref, encoded_ref, igrad_ref,
    mask_ref, first_ref, last_ref, stats_out, stats_ref, sums_ref, slabs_ref,
    own_part, far_part, core_in, send1, in1, send2, in2, in3,
    tm_total, core_sum, x_sums, x_total, z_sum,
    local_sem, move_send, move_recv, stat_send, stat_recv,
    send_sem, recv_sem, pair_send, pair_recv,
):
    frames, places, channels = loaded_ref.shape
    blocks = own_part.shape[1]
    part, piece, lanes = blocks // 4, blocks // 16, channels // 2
    per_row = blocks // 3
    slabs = 8

    dp, tm = lax.axis_index("dp"), lax.axis_index("tm")
    core, x, y = dp % 2, dp // 4, tm % 4
    z = (dp // 2) % 2 * 2 + tm // 4
    here = (x, y, z)

    def device(place, its_core):
        return ((place[0] * 2 + place[2] // 2) * 2 + its_core, (place[2] % 2) * 4 + place[1])

    def along(axis, off):
        place = list(here)
        place[axis] = (here[axis] + off) % 4
        return place[axis], device(place, core)

    other = device(here, 1 - core)
    across = device((x, y, (z + 2) % 4), core)
    tm_peers = [(dp, (tm + off) % slabs) for off in range(1, slabs)]
    axis_peers = [along(axis, off)[1] for axis in (0, 1, 2) for off in (1, 2, 3)]
    before, after = (dp, (tm + slabs - 1) % slabs), (dp, (tm + 1) % slabs)
    has_before, has_after = tm > 0, tm < slabs - 1

    barrier = pltpu.get_barrier_semaphore()
    greeted = [other] + axis_peers + tm_peers
    for peer in greeted:
        pl.semaphore_signal(barrier, inc=1, device_id=peer, device_id_type=MESH)

    loads = [
        pltpu.make_async_copy(src, dst, local_sem.at[i])
        for i, (src, dst) in enumerate(
            ((loaded_hbm, loaded_ref), (cot_hbm, cot_ref), (weight_hbm, weight_ref))
        )
    ]
    for load in loads:
        load.start()
    pl.semaphore_wait(barrier, len(greeted))

    def remote(src, dst, send_at, recv_at, peer):
        return pltpu.make_async_remote_copy(
            src_ref=src, dst_ref=dst, send_sem=send_at, recv_sem=recv_at,
            device_id=peer, device_id_type=MESH,
        )

    def send(*arguments):
        copy = remote(*arguments)
        copy.start()
        return copy

    halo = remote(cot_hbm.at[pl.ds(0, 2)], next_ref, move_send.at[0], move_recv.at[0], before)
    bulk = remote(loaded_hbm, arrived_ref, move_send.at[1], move_recv.at[1], before)
    tails = remote(tail_out, tail_ref, move_send.at[2], move_recv.at[2], after)

    @pl.when(has_before)
    def _():
        halo.start()
        bulk.start()

    @pl.when(tm == slabs - 1)
    def _():
        next_ref[...] = jnp.zeros_like(next_ref)
        arrived_ref[...] = jnp.zeros_like(arrived_ref)

    @pl.when(tm == 0)
    def _():
        tail_ref[...] = jnp.zeros_like(tail_ref)

    own_start, own_length = start_of(len_ref, slabs, tm), length_of(len_ref, slabs, tm)
    next_start, next_length = own_start + own_length, length_of(len_ref, slabs, tm + 1)
    frame_total = start_of(len_ref, slabs, slabs)
    area = res_ref[0, 0] * res_ref[0, 1] * width
    count = (frame_total * area).astype(F32)
    mask_ref[...] = cells(res_ref, cols, (places, channels)).astype(F32)
    first, last = col_masks(cols, (places, channels))
    first_ref[...] = first
    last_ref[...] = last
    zero = jnp.zeros((8, channels), F32)
    row = lax.broadcasted_iota(jnp.int32, (8, channels), 0)

    loads[0].wait()

    def fold(value):
        return jnp.sum(value.reshape(places // 8, 8, channels), axis=0)

    def over_groups(total):
        line = jnp.sum(total, axis=0, keepdims=True)
        return group_sum(jnp.broadcast_to(line, (8, channels)), width)

    def add_up(f, total):
        held = (f < own_length).astype(F32)
        return total + fold(loaded_ref[f].astype(F32) * (mask_ref[...] * held))

    own_mean = over_groups(lax.fori_loop(0, frames, add_up, zero)) / (own_length * area).astype(F32)
    mean_row = own_mean[0:1]

    def spread(f, total):
        held = (f < own_length).astype(F32)
        apart = (loaded_ref[f].astype(F32) - mean_row) * (mask_ref[...] * held)
        return total + fold(apart * apart)

    squares = over_groups(lax.fori_loop(0, frames, spread, zero))
    stats_out[...] = jnp.where(row == 0, own_mean, squares)
    stats_ref[tm] = stats_out[...]
    stats_shares = [
        send(stats_out, stats_ref.at[tm], stat_send.at[i], stat_recv.at[i], peer)
        for i, peer in enumerate(tm_peers)
    ]
    for k in range(2):
        offset = tm * frames + frames - 2 + k - own_start
        usable = (offset >= 0) & (offset < own_length)
        picked = loaded_ref[jnp.clip(offset, 0, frames - 1)]
        tail_out[k] = jnp.where(usable, picked, jnp.zeros_like(picked))

    @pl.when(has_after)
    def _():
        tails.start()

    loads[2].wait()

    def turn(block, _):
        for k in range(3):
            turned_ref[block, k * channels : (k + 1) * channels, :] = weight_ref[
                block, (2 - k) * channels : (3 - k) * channels, :
            ].T
        return 0

    lax.fori_loop(0, 9, turn, 0)
    blank = jnp.zeros((cols, 3 * channels), BF16)

    def place(frame, value):
        alive = (tm * frames + frame < frame_total).astype(F32)
        value = value.astype(F32) * (mask_ref[...] * alive)
        back_cat[frame, 0] = blank
        back_cat[frame, rows + 1] = blank
        lay_out(back_cat, frame, value, rows, cols, first_ref[...], last_ref[...])
        return value

    loads[1].wait()

    def own_grad(f, _):
        value = place(f, cot_ref[f])
        grad_ref[pl.ds(pl.multiple_of(f * places, places), places)] = value.astype(BF16)
        return 0

    lax.fori_loop(0, frames, own_grad, 0)

    def convolve(source, factor, f, back):
        total = jnp.zeros((places, channels), F32)
        for d in range(3):
            for r in range(3):
                at = (f + 2 - d, 2 - r) if back else (f + d, r)
                lines = source[at[0], at[1] : at[1] + rows].reshape(places, 3 * channels)
                total = total + jnp.dot(lines, factor[3 * d + r], preferred_element_type=F32)
        return total * (mask_ref[...] * (tm * frames + f < frame_total).astype(F32))

    def back_sweep(f, _):
        agrad_ref[f] = convolve(back_cat, turned_ref, f, True)
        return 0

    lax.fori_loop(0, frames - 2, back_sweep, 0)

    @pl.when(has_after)
    def _():
        halo.wait_recv()

    for k in range(2):
        place(frames + k, next_ref[k])
    lax.fori_loop(frames - 2, frames, back_sweep, 0)

    for copy in stats_shares:
        copy.wait()
    counts = [(len_ref[0, i] * area).astype(F32) for i in range(slabs)]
    mean = jnp.zeros((1, channels), F32)
    for i in range(slabs):
        mean = mean + counts[i] * stats_ref[i, 0:1]
    mean = mean / count
    squares = jnp.zeros((1, channels), F32)
    for i in range(slabs):
        apart = stats_ref[i, 0:1] - mean
        squares = squares + stats_ref[i, 1:2] + counts[i] * (apart * apart)
    root = lax.rsqrt(squares / count + EPSILON)
    gain, bias = gain_ref[...], bias_ref[...]

    def activate(slot, frame_id, value):
        alive = ((frame_id >= 0) & (frame_id < frame_total)).astype(F32)
        live = mask_ref[...] * alive
        normed = (value.astype(F32) * live - mean) * live * root
        pre = normed * gain + bias
        gate = 1.0 / (1.0 + jnp.exp(-pre))
        act = (pre * gate * live).astype(BF16).astype(F32)
        cat_ref[slot, 0] = blank
        cat_ref[slot, rows + 1] = blank
        lay_out(cat_ref, slot, act, rows, cols, first_ref[...], last_ref[...])
        return normed, pre, gate

    @pl.when(has_before)
    def _():
        tails.wait_recv()

    for k in range(2):
        frame_id = tm * frames + k - 2
        offset = frame_id - own_start
        usable = (offset >= 0) & (offset < own_length)
        picked = jnp.where(usable, loaded_ref[jnp.clip(offset, 0, frames - 1)], tail_ref[k])
        activate(k, frame_id, picked)

    @pl.when(has_after)
    def _():
        bulk.wait_recv()

    def own_frame(f, sums):
        frame_id = tm * frames + f
        offset = frame_id - own_start
        later = frame_id - next_start
        picked = jnp.where(
            offset < own_length,
            loaded_ref[jnp.clip(offset, 0, frames - 1)],
            arrived_ref[jnp.clip(later, 0, frames - 1)],
        )
        normed, pre, gate = activate(f + 2, frame_id, picked)
        pre_grad = agrad_ref[f] * gate * (1.0 + pre * (1.0 - gate))
        normed_ref[f] = normed
        agrad_ref[f] = pre_grad * gain
        return sums[0] + fold(pre_grad * normed), sums[1] + fold(pre_grad)

    gain_sum, bias_sum = lax.fori_loop(0, frames, own_frame, (zero, zero))
    sums_ref[...] = jnp.where(
        row == 0,
        jnp.sum(gain_sum, axis=0, keepdims=True),
        jnp.where(row == 1, jnp.sum(bias_sum, axis=0, keepdims=True), 0.0),
    )
    slabs_ref[tm] = sums_ref[...]
    shares = [
        send(sums_ref, slabs_ref.at[tm], pair_send.at[i], pair_recv.at[i], peer)
        for i, peer in enumerate(tm_peers)
    ]

    order = [(k % 3, (k + 1) % 3, (k + 2) % 3) for k in range(3)]
    own_lanes = pl.ds(pl.multiple_of(core * lanes, lanes), lanes)

    def spread_out(stage, k, axis, source, target):
        row_of = []
        for off in (1, 2, 3):
            there, peer = along(axis, off)
            row_of.append(
                send(
                    source(there), target(off - 1),
                    send_sem.at[stage, k, off - 1], recv_sem.at[stage, k, off - 1], peer,
                )
            )
        return row_of

    def kernel_part(k):
        for r in range(3):
            lines = cat_ref[k : k + frames, r : r + rows].reshape(frames * places, 3 * channels)
            product = lax.dot_general(
                lines, grad_ref[...], (((0,), (0,)), ((), ())), preferred_element_type=F32
            ).reshape(per_row, 16, channels)
            low, high = product[..., :lanes], product[..., lanes:]
            at = slice(r * per_row, (r + 1) * per_row)
            own_part[k, at] = jnp.where(core == 0, low, high)
            far_part[k, at] = jnp.where(core == 0, high, low).astype(BF16)
        return send(
            far_part.at[k], core_in.at[k], send_sem.at[0, k, 0], recv_sem.at[0, k, 0], other
        )

    def first_stage(k, half):
        half.wait()

        def add_half(b, _):
            at = pl.ds(b * 4, 4)
            both = own_part[k, at] + core_in[k, at].astype(F32)
            own_part[k, at] = both
            send1[k, at] = both.astype(BF16)
            return 0

        lax.fori_loop(0, blocks // 4, add_half, 0)
        return spread_out(
            1, k, order[k][0],
            lambda there: send1.at[k, pl.ds(there * part, part)],
            lambda i: in1.at[k, i],
        )

    def second_stage(k, copies):
        for copy in copies:
            copy.wait()
        base = here[order[k][0]] * part

        def add_first(b, _):
            at = pl.ds(b * 3, 3)
            own = own_part[k, pl.ds(base + b * 3, 3)]
            for i in range(3):
                own = own + in1[k, i, at].astype(F32)
            send2[k, at] = own.astype(BF16)
            return 0

        lax.fori_loop(0, part // 3, add_first, 0)
        return spread_out(
            2, k, order[k][1],
            lambda there: send2.at[k, pl.ds(there * piece, piece)],
            lambda i: in2.at[k, i],
        )

    def third_stage(k, copies):
        for copy in copies:
            copy.wait()
        base = here[order[k][1]] * piece
        spot = here[order[k][2]]

        def add_second(b, _):
            at = pl.ds(b * 3, 3)
            own = send2[k, pl.ds(base + b * 3, 3)].astype(F32)
            for i in range(3):
                own = own + in2[k, i, at].astype(F32)
            in3[k, spot, at] = own.astype(BF16)
            return 0

        lax.fori_loop(0, piece // 3, add_second, 0)
        return spread_out(
            3, k, order[k][2], lambda there: in3.at[k, spot], lambda i: in3.at[k, spot]
        )

    def fourth_stage(k, copies):
        for copy in copies:
            copy.wait()
        base = here[order[k][0]] * part + here[order[k][1]] * piece

        def add_third(b, _):
            at = pl.ds(b * 3, 3)
            own = in3[k, 0, at].astype(F32)
            for i in range(1, 4):
                own = own + in3[k, i, at].astype(F32)
            total_ref[k, pl.ds(base + b * 3, 3), :, own_lanes] = own.astype(BF16)
            return 0

        lax.fori_loop(0, piece // 3, add_third, 0)
        spot = total_ref.at[k, pl.ds(base, piece), :, own_lanes]
        return spread_out(4, k, order[k][1], lambda there: spot, lambda i: spot)

    def fifth_stage(k, copies):
        for copy in copies:
            copy.wait()
        spot = total_ref.at[k, pl.ds(here[order[k][0]] * part, part), :, own_lanes]
        return spread_out(5, k, order[k][0], lambda there: spot, lambda i: spot)

    def sixth_stage(k, copies):
        for copy in copies:
            copy.wait()
        spot = total_ref.at[k, :, :, own_lanes]
        return send(spot, spot, send_sem.at[6, k, 0], recv_sem.at[6, k, 0], other)

    def forward_sweep(f, _):
        encoded_ref[f] = convolve(cat_ref, weight_ref, f, False).astype(BF16)
        return 0

    half0 = kernel_part(0)
    half1 = kernel_part(1)
    stage0 = first_stage(0, half0)
    half2 = kernel_part(2)
    stage1 = first_stage(1, half1)

    for copy in shares:
        copy.wait()
    total = slabs_ref[0]
    for i in range(1, slabs):
        total = total + slabs_ref[i]
    tm_total[...] = total
    core_copy = send(tm_total, core_sum, pair_send.at[7], pair_recv.at[7], other)

    lax.fori_loop(0, 2, forward_sweep, 0)
    stage2 = first_stage(2, half2)

    core_copy.wait()
    x_sums[x] = tm_total[...] + core_sum[...]
    x_copies = [
        send(x_sums.at[x], x_sums.at[x], pair_send.at[7 + off], pair_recv.at[7 + off], along(0, off)[1])
        for off in (1, 2, 3)
    ]
    lax.fori_loop(2, 5, forward_sweep, 0)
    stage0 = second_stage(0, stage0)
    lax.fori_loop(5, frames, forward_sweep, 0)
    stage1 = second_stage(1, stage1)
    encoded_copy = pltpu.make_async_copy(encoded_ref, encoded_hbm, local_sem.at[3])
    encoded_copy.start()

    for copy in x_copies:
        copy.wait()
    x_total[...] = x_sums[0] + x_sums[1] + x_sums[2] + x_sums[3]
    z_copy = send(x_total, z_sum, pair_send.at[11], pair_recv.at[11], across)

    stage0 = third_stage(0, stage0)
    stage2 = second_stage(2, stage2)
    stage1 = third_stage(1, stage1)

    shares_of = group_sum(tm_total[...] * gain, width) / count
    mean_part, along_part = shares_of[1:2], shares_of[0:1]

    def finish(f, _):
        live = mask_ref[...] * (tm * frames + f < frame_total).astype(F32)
        inner = agrad_ref[f] - mean_part - normed_ref[f] * along_part
        igrad_ref[f] = (inner * root * live).astype(BF16)
        return 0

    lax.fori_loop(0, frames, finish, 0)
    igrad_copy = pltpu.make_async_copy(igrad_ref, igrad_hbm, local_sem.at[4])
    igrad_copy.start()

    stage0 = fourth_stage(0, stage0)
    stage2 = third_stage(2, stage2)
    stage1 = fourth_stage(1, stage1)
    z_copy.wait()
    pair_ref[...] = x_total[...] + z_sum[...]
    stage0 = fifth_stage(0, stage0)
    stage2 = fourth_stage(2, stage2)
    stage1 = fifth_stage(1, stage1)
    stage2 = fifth_stage(2, stage2)
    ends = [sixth_stage(0, stage0), sixth_stage(1, stage1), sixth_stage(2, stage2)]
    for copy in ends:
        copy.wait()
    encoded_copy.wait()
    igrad_copy.wait()

    @pl.when(has_before)
    def _():
        halo.wait_send()
        bulk.wait_send()

    @pl.when(has_after)
    def _():
        tails.wait_send()


def body(loaded, lengths, resolution, weight, norm_gain, norm_bias, cotangent):
    frames, rows, cols, channels = loaded.shape[1:]
    places, width, lanes = rows * cols, channels // GROUPS, channels // 2
    slabs = lax.axis_size("tm")
    shape = jax.ShapeDtypeStruct
    slab = (frames, places, channels)
    blocks = 9 * channels // 16
    part, piece = blocks // 4, blocks // 16

    def tiles(*lead, kind=BF16):
        return pltpu.VMEM(lead + (16, lanes), kind)

    small = pltpu.VMEM((8, channels), F32)
    plane = pltpu.VMEM((places, channels), F32)
    cat = pltpu.VMEM((frames + 2, rows + 2, cols, 3 * channels), BF16)
    dma = pltpu.SemaphoreType.DMA
    encoded, igrad, total, pair = pl.pallas_call(
        functools.partial(section_kernel, rows, cols, width),
        out_shape=(
            shape(slab, BF16),
            shape(slab, BF16),
            shape((3, blocks, 16, channels), BF16),
            shape((8, channels), F32),
        ),
        in_specs=[SMEM, SMEM, ANY, ANY, ANY, VMEM, VMEM],
        out_specs=(ANY, ANY, VMEM, VMEM),
        scratch_shapes=[
            pltpu.VMEM(slab, BF16),
            pltpu.VMEM(slab, BF16),
            pltpu.VMEM(slab, BF16),
            pltpu.VMEM((2, places, channels), BF16),
            pltpu.VMEM((2, places, channels), BF16),
            pltpu.VMEM((2, places, channels), BF16),
            pltpu.VMEM((9, 3 * channels, channels), BF16),
            pltpu.VMEM((9, 3 * channels, channels), BF16),
            cat,
            cat,
            pltpu.VMEM((frames * places, channels), BF16),
            pltpu.VMEM(slab, F32),
            pltpu.VMEM(slab, F32),
            pltpu.VMEM(slab, BF16),
            pltpu.VMEM(slab, BF16),
            plane,
            plane,
            plane,
            small,
            pltpu.VMEM((slabs, 8, channels), F32),
            small,
            pltpu.VMEM((slabs, 8, channels), F32),
            tiles(3, blocks, kind=F32),
            tiles(3, blocks),
            tiles(3, blocks),
            tiles(3, blocks),
            tiles(3, 3, part),
            tiles(3, part),
            tiles(3, 3, piece),
            tiles(3, 4, piece),
            small,
            small,
            pltpu.VMEM((4, 8, channels), F32),
            small,
            small,
            dma((5,)),
            dma((3,)),
            dma((3,)),
            dma((7,)),
            dma((7,)),
            dma((7, 3, 3)),
            dma((7, 3, 3)),
            dma((12,)),
            dma((12,)),
        ],
        compiler_params=params(58, collective_id=1, has_side_effects=True),
    )(
        lengths,
        resolution,
        loaded.reshape(slab),
        cotangent.reshape(slab),
        weight.reshape(9, 3 * channels, channels),
        norm_gain.reshape(1, channels),
        norm_bias.reshape(1, channels),
    )
    scale = 1.0 / math.sqrt(lax.axis_size("dp") * slabs * frames * places)
    whole = (1, frames, rows, cols, channels)
    return (
        encoded.reshape(whole),
        igrad.reshape(whole),
        total.reshape(27, channels, channels).astype(F32) * scale,
        pair[0] * scale,
        pair[1] * scale,
    )


def solution(mesh):
    slab = P("dp", "tm", None, None, None)
    return jax.shard_map(
        body,
        mesh=mesh,
        in_specs=(slab, P("dp", None), P("dp", None), P(), P(), P(), slab),
        out_specs=(slab, slab, P(), P(), P()),
        check_vma=False,
    )
```

time: 265 us -> 102 us (0.38)
  waiting for transfers between devices: 77.9 us -> 0 us
  blocking collectives: 68.4 us -> 0 us
  Pallas kernels: 74.5 us -> 92.1 us
  between operations: 14.2 us -> 0.66 us
  local copies, waits for them, and re-layouts: 14.1 us -> 1.95 us
  starting transfers between devices: 8.54 us -> 0 us
    psum x1 -> x0, waiting for transfers between devices: 77.9 us -> none  [body(): kernel_sum, pair_sum = lax.psum((kernel_part, sums[:2]), ('dp', 'tm'))]
    psum x1 -> x0, blocking collectives: 68.4 us -> none  [body(): kernel_sum, pair_sum = lax.psum((kernel_part, sums[:2]), ('dp', 'tm'))]
    pallas_call x6 -> x1, Pallas kernels: 74.5 us -> 92.1 us  [body(): pl.pallas_call(functools.partial(section_kernel, rows, cols, width), out_...]
    unnamed x36 -> x6, local copies, waits for them, and re-layouts: 12.5 us -> 1.95 us
    ppermute x3 -> x0, starting transfers between devices: 8.5 us -> none  [shifted(): return lax.ppermute(block, axis, route)]
  transfers between devices with their start and end apart: 4 -> 0, of which waited for: 1 -> 0; matrix products, arithmetic and copies ran while one was open for 1% -> 0% of each run, Pallas kernels for 18% -> 0%
where the time goes in v3:
time: 102 us
  Pallas kernels  92.1 us (90%)
  other arithmetic  7.41 us (7%)
  local copies, waits for them, and re-layouts  1.95 us (2%)
    pallas_call x1, Pallas kernels, body(): pl.pallas_call(functools.partial(section_kernel, rows, cols, width), out_...  92.1 us
    mul x1, other arithmetic, body(): total.reshape(27, channels, channels).astype(F32) * scale  5.98 us

profile of v3, /device:TPU:1, one launch (start us, length us, event | category | flops | bytes accessed | tf_op | source)
XLA Modules:
  0.0 102.1 jit_solution(5913404081618170489)
XLA Ops:
  0.6 92.1 %shard_map.110 = (bf16[8,256,256]{2,1,0:T(8,128)(2,1)}, bf16[8,256,256]{2,1,0:T(8,128)(2,1)}, bf16[3,144,16,256]{3,2,1,0:T(8,128)(2,1)}, f32[8,256]{1,0:T(8,128)}) custom-call(s32[1,8]{1,0:T(1,128)} %len_ref.1, s32[1,2]{1,0:T(1,128)} %res_ref.1, bf16[8,256,256]{2,1,0:T(8,128)(2,1)} %bitcast.14, bf16[8,256,256]{2,1,0:T(8,128)(2,1)} %bitcast.15, ...), custom_call_target="tpu_custom_call" | custom-call | tf_op jit(solution)/shard_map/pallas_call | solution.py:535
  92.8 0.0 copy-start.1
  92.8 0.0 copy-start
  92.8 1.4 %slice_multiply_fusion = (f32[1,256]{1,0:T(1,128)}, f32[1,256]{1,0:T(1,128)}) fusion(f32[8,256]{1,0:T(8,128)} %get-tuple-element.12), kind=kLoop, calls=%fused_computation.1 | loop fusion | flops 512 | bytes 4096 | tf_op jit(solution)/shard_map/mul | solution.py:608
  94.2 6.0 %convert_multiply_fusion = f32[3,144,16,256]{3,2,1,0:T(8,128)} fusion(bf16[3,144,16,256]{3,2,1,0:T(8,128)(2,1)} %get-tuple-element.11), kind=kLoop, calls=%fused_computation | loop fusion | flops 3538944 | bytes 10616832 | tf_op jit(solution)/shard_map/mul | solution.py:606
  100.2 0.0 copy-done.1
  100.2 1.0 copy.14
  101.2 0.0 copy-done
  101.2 1.0 copy.15
Async XLA Ops:
  92.8 7.4 %copy-start.1 = (bf16[8,256,256]{2,1,0:T(8,128)(2,1)S(1)}, bf16[8,256,256]{2,1,0:T(8,128)(2,1)}, u32[]{:S(2)}) copy-start(bf16[8,256,256]{2,1,0:T(8,128)(2,1)} %get-tuple-element.9) | copy-start | bytes 3145732
  92.8 8.4 %copy-start = (bf16[8,256,256]{2,1,0:T(8,128)(2,1)S(1)}, bf16[8,256,256]{2,1,0:T(8,128)(2,1)}, u32[]{:S(2)}) copy-start(bf16[8,256,256]{2,1,0:T(8,128)(2,1)} %get-tuple-element.10) | copy-start | bytes 3145732

commit v4 on v3

--- a/solution.py
+++ b/solution.py
@@ -72,11 +72,11 @@
 def section_kernel(
     rows, cols, width,
     len_ref, res_ref, loaded_hbm, cot_hbm, weight_hbm, gain_ref, bias_ref,
-    encoded_hbm, igrad_hbm, total_ref, pair_ref,
-    loaded_ref, arrived_ref, cot_ref, next_ref, tail_out, tail_ref, weight_ref, turned_ref,
+    encoded_hbm, igrad_hbm, total_hbm, pair_ref,
+    loaded_ref, leaving_ref, arrived_ref, cot_ref, next_ref, tail_out, tail_ref, weight_ref, turned_ref,
     back_cat, cat_ref, grad_ref, agrad_ref, normed_ref, encoded_ref, igrad_ref,
     mask_ref, first_ref, last_ref, stats_out, stats_ref, sums_ref, slabs_ref,
-    own_part, far_part, core_in, send1, in1, send2, in2, in3,
+    total_ref, own_part, far_sum, far_part, core_in, send1, in1, send2, in2, in3,
     tm_total, core_sum, x_sums, x_total, z_sum,
     local_sem, move_send, move_recv, stat_send, stat_recv,
     send_sem, recv_sem, pair_send, pair_recv,
@@ -85,6 +85,7 @@
     blocks = own_part.shape[1]
     part, piece, lanes = blocks // 4, blocks // 16, channels // 2
     per_row = blocks // 3
+    early = frames - 2
     slabs = 8
 
     dp, tm = lax.axis_index("dp"), lax.axis_index("tm")
@@ -120,7 +121,6 @@
     ]
     for load in loads:
         load.start()
-    pl.semaphore_wait(barrier, len(greeted))
 
     def remote(src, dst, send_at, recv_at, peer):
         return pltpu.make_async_remote_copy(
@@ -133,14 +133,17 @@
         copy.start()
         return copy
 
-    halo = remote(cot_hbm.at[pl.ds(0, 2)], next_ref, move_send.at[0], move_recv.at[0], before)
-    bulk = remote(loaded_hbm, arrived_ref, move_send.at[1], move_recv.at[1], before)
-    tails = remote(tail_out, tail_ref, move_send.at[2], move_recv.at[2], after)
-
-    @pl.when(has_before)
-    def _():
-        halo.start()
-        bulk.start()
+    halo = remote(
+        cot_hbm.at[pl.ds(0, 2)], next_ref, move_send.at[frames], move_recv.at[frames], before
+    )
+    tails = remote(
+        tail_out, tail_ref, move_send.at[frames + 1], move_recv.at[frames + 1], after
+    )
+
+    def moved(f):
+        return remote(
+            leaving_ref.at[f], arrived_ref.at[f], move_send.at[f], move_recv.at[f], before
+        )
 
     @pl.when(tm == slabs - 1)
     def _():
@@ -152,7 +155,6 @@
         tail_ref[...] = jnp.zeros_like(tail_ref)
 
     own_start, own_length = start_of(len_ref, slabs, tm), length_of(len_ref, slabs, tm)
-    next_start, next_length = own_start + own_length, length_of(len_ref, slabs, tm + 1)
     frame_total = start_of(len_ref, slabs, slabs)
     area = res_ref[0, 0] * res_ref[0, 1] * width
     count = (frame_total * area).astype(F32)
@@ -187,19 +189,37 @@
     squares = over_groups(lax.fori_loop(0, frames, spread, zero))
     stats_out[...] = jnp.where(row == 0, own_mean, squares)
     stats_ref[tm] = stats_out[...]
-    stats_shares = [
-        send(stats_out, stats_ref.at[tm], stat_send.at[i], stat_recv.at[i], peer)
-        for i, peer in enumerate(tm_peers)
-    ]
     for k in range(2):
         offset = tm * frames + frames - 2 + k - own_start
         usable = (offset >= 0) & (offset < own_length)
         picked = loaded_ref[jnp.clip(offset, 0, frames - 1)]
         tail_out[k] = jnp.where(usable, picked, jnp.zeros_like(picked))
 
+
+    def pack(f, _):
+        offset = (tm - 1) * frames + f - own_start
+        usable = (offset >= 0) & (offset < own_length)
+        picked = loaded_ref[jnp.clip(offset, 0, frames - 1)]
+        leaving_ref[f] = jnp.where(usable, picked, jnp.zeros_like(picked))
+        return 0
+
+    lax.fori_loop(0, frames, pack, 0)
+
+    pl.semaphore_wait(barrier, len(greeted))
+    stats_shares = [
+        send(stats_out, stats_ref.at[tm], stat_send.at[i], stat_recv.at[i], peer)
+        for i, peer in enumerate(tm_peers)
+    ]
+
     @pl.when(has_after)
     def _():
         tails.start()
+
+    @pl.when(has_before)
+    def _():
+        for f in range(frames):
+            moved(f).start()
+        halo.start()
 
     loads[2].wait()
 
@@ -244,14 +264,6 @@
         return 0
 
     lax.fori_loop(0, frames - 2, back_sweep, 0)
-
-    @pl.when(has_after)
-    def _():
-        halo.wait_recv()
-
-    for k in range(2):
-        place(frames + k, next_ref[k])
-    lax.fori_loop(frames - 2, frames, back_sweep, 0)
 
     for copy in stats_shares:
         copy.wait()
@@ -277,7 +289,7 @@
         cat_ref[slot, 0] = blank
         cat_ref[slot, rows + 1] = blank
         lay_out(cat_ref, slot, act, rows, cols, first_ref[...], last_ref[...])
-        return normed, pre, gate
+        return normed
 
     @pl.when(has_before)
     def _():
@@ -290,36 +302,28 @@
         picked = jnp.where(usable, loaded_ref[jnp.clip(offset, 0, frames - 1)], tail_ref[k])
         activate(k, frame_id, picked)
 
-    @pl.when(has_after)
-    def _():
-        bulk.wait_recv()
-
-    def own_frame(f, sums):
+    def own_frame(f, _):
+        @pl.when(has_after)
+        def _():
+            moved(f).wait_recv()
+
         frame_id = tm * frames + f
         offset = frame_id - own_start
-        later = frame_id - next_start
         picked = jnp.where(
             offset < own_length,
             loaded_ref[jnp.clip(offset, 0, frames - 1)],
-            arrived_ref[jnp.clip(later, 0, frames - 1)],
-        )
-        normed, pre, gate = activate(f + 2, frame_id, picked)
+            arrived_ref[f],
+        )
+        normed_ref[f] = activate(f + 2, frame_id, picked)
+        return 0
+
+    def through(f, sums):
+        normed = normed_ref[f]
+        pre = normed * gain + bias
+        gate = 1.0 / (1.0 + jnp.exp(-pre))
         pre_grad = agrad_ref[f] * gate * (1.0 + pre * (1.0 - gate))
-        normed_ref[f] = normed
         agrad_ref[f] = pre_grad * gain
         return sums[0] + fold(pre_grad * normed), sums[1] + fold(pre_grad)
-
-    gain_sum, bias_sum = lax.fori_loop(0, frames, own_frame, (zero, zero))
-    sums_ref[...] = jnp.where(
-        row == 0,
-        jnp.sum(gain_sum, axis=0, keepdims=True),
-        jnp.where(row == 1, jnp.sum(bias_sum, axis=0, keepdims=True), 0.0),
-    )
-    slabs_ref[tm] = sums_ref[...]
-    shares = [
-        send(sums_ref, slabs_ref.at[tm], pair_send.at[i], pair_recv.at[i], peer)
-        for i, peer in enumerate(tm_peers)
-    ]
 
     order = [(k % 3, (k + 1) % 3, (k + 2) % 3) for k in range(3)]
     own_lanes = pl.ds(pl.multiple_of(core * lanes, lanes), lanes)
@@ -336,16 +340,28 @@
             )
         return row_of
 
+    def product(k, r, begin, end):
+        lines = cat_ref[k + begin : k + end, r : r + rows].reshape(-1, 3 * channels)
+        both = lax.dot_general(
+            lines,
+            grad_ref[begin * places : end * places],
+            (((0,), (0,)), ((), ())),
+            preferred_element_type=F32,
+        ).reshape(per_row, 16, channels)
+        low, high = both[..., :lanes], both[..., lanes:]
+        return jnp.where(core == 0, low, high), jnp.where(core == 0, high, low)
+
+    def early_part(k):
+        for r in range(3):
+            at = slice(r * per_row, (r + 1) * per_row)
+            own_part[k, at], far_sum[k, at] = product(k, r, 0, early)
+
     def kernel_part(k):
         for r in range(3):
-            lines = cat_ref[k : k + frames, r : r + rows].reshape(frames * places, 3 * channels)
-            product = lax.dot_general(
-                lines, grad_ref[...], (((0,), (0,)), ((), ())), preferred_element_type=F32
-            ).reshape(per_row, 16, channels)
-            low, high = product[..., :lanes], product[..., lanes:]
             at = slice(r * per_row, (r + 1) * per_row)
-            own_part[k, at] = jnp.where(core == 0, low, high)
-            far_part[k, at] = jnp.where(core == 0, high, low).astype(BF16)
+            own, far = product(k, r, early, frames)
+            own_part[k, at] = own_part[k, at] + own
+            far_part[k, at] = (far_sum[k, at] + far).astype(BF16)
         return send(
             far_part.at[k], core_in.at[k], send_sem.at[0, k, 0], recv_sem.at[0, k, 0], other
         )
@@ -423,28 +439,71 @@
         spot = total_ref.at[k, pl.ds(base, piece), :, own_lanes]
         return spread_out(4, k, order[k][1], lambda there: spot, lambda i: spot)
 
+    def region(k, there):
+        return total_ref.at[k, pl.ds(there * part, part), :, own_lanes]
+
+    def to_core(k, there, i):
+        spot = region(k, there)
+        return send(spot, spot, send_sem.at[6, k, i], recv_sem.at[6, k, i], other)
+
     def fifth_stage(k, copies):
         for copy in copies:
             copy.wait()
-        spot = total_ref.at[k, pl.ds(here[order[k][0]] * part, part), :, own_lanes]
-        return spread_out(5, k, order[k][0], lambda there: spot, lambda i: spot)
-
-    def sixth_stage(k, copies):
-        for copy in copies:
-            copy.wait()
-        spot = total_ref.at[k, :, :, own_lanes]
-        return send(spot, spot, send_sem.at[6, k, 0], recv_sem.at[6, k, 0], other)
+        mine = here[order[k][0]]
+        row_of = spread_out(
+            5, k, order[k][0], lambda there: region(k, mine), lambda i: region(k, mine)
+        )
+        return row_of, [to_core(k, mine, 0)]
+
+    def sixth_stage(k, off, copies):
+        copies[0][off - 1].wait()
+        copies[1].append(to_core(k, (here[order[k][0]] + 4 - off) % 4, off))
 
     def forward_sweep(f, _):
         encoded_ref[f] = convolve(cat_ref, weight_ref, f, False).astype(BF16)
         return 0
+
+    def take_in(f, _):
+        own_frame(f, 0)
+        forward_sweep(f, 0)
+        return 0
+
+    lax.fori_loop(0, early, take_in, 0)
+    for k in range(3):
+        early_part(k)
+    lax.fori_loop(early, frames, own_frame, 0)
 
     half0 = kernel_part(0)
     half1 = kernel_part(1)
     stage0 = first_stage(0, half0)
     half2 = kernel_part(2)
     stage1 = first_stage(1, half1)
-
+    lax.fori_loop(early, frames, forward_sweep, 0)
+    encoded_copy = pltpu.make_async_copy(encoded_ref, encoded_hbm, local_sem.at[3])
+    encoded_copy.start()
+    stage2 = first_stage(2, half2)
+
+    @pl.when(has_after)
+    def _():
+        halo.wait_recv()
+
+    for k in range(2):
+        place(frames + k, next_ref[k])
+    lax.fori_loop(frames - 2, frames, back_sweep, 0)
+    gain_sum, bias_sum = lax.fori_loop(0, frames, through, (zero, zero))
+    sums_ref[...] = jnp.where(
+        row == 0,
+        jnp.sum(gain_sum, axis=0, keepdims=True),
+        jnp.where(row == 1, jnp.sum(bias_sum, axis=0, keepdims=True), 0.0),
+    )
+    slabs_ref[tm] = sums_ref[...]
+    shares = [
+        send(sums_ref, slabs_ref.at[tm], pair_send.at[i], pair_recv.at[i], peer)
+        for i, peer in enumerate(tm_peers)
+    ]
+
+    stage0 = second_stage(0, stage0)
+    stage1 = second_stage(1, stage1)
     for copy in shares:
         copy.wait()
     total = slabs_ref[0]
@@ -452,9 +511,9 @@
         total = total + slabs_ref[i]
     tm_total[...] = total
     core_copy = send(tm_total, core_sum, pair_send.at[7], pair_recv.at[7], other)
-
-    lax.fori_loop(0, 2, forward_sweep, 0)
-    stage2 = first_stage(2, half2)
+    stage0 = third_stage(0, stage0)
+    stage2 = second_stage(2, stage2)
+    stage1 = third_stage(1, stage1)
 
     core_copy.wait()
     x_sums[x] = tm_total[...] + core_sum[...]
@@ -462,22 +521,6 @@
         send(x_sums.at[x], x_sums.at[x], pair_send.at[7 + off], pair_recv.at[7 + off], along(0, off)[1])
         for off in (1, 2, 3)
     ]
-    lax.fori_loop(2, 5, forward_sweep, 0)
-    stage0 = second_stage(0, stage0)
-    lax.fori_loop(5, frames, forward_sweep, 0)
-    stage1 = second_stage(1, stage1)
-    encoded_copy = pltpu.make_async_copy(encoded_ref, encoded_hbm, local_sem.at[3])
-    encoded_copy.start()
-
-    for copy in x_copies:
-        copy.wait()
-    x_total[...] = x_sums[0] + x_sums[1] + x_sums[2] + x_sums[3]
-    z_copy = send(x_total, z_sum, pair_send.at[11], pair_recv.at[11], across)
-
-    stage0 = third_stage(0, stage0)
-    stage2 = second_stage(2, stage2)
-    stage1 = third_stage(1, stage1)
-
     shares_of = group_sum(tm_total[...] * gain, width) / count
     mean_part, along_part = shares_of[1:2], shares_of[0:1]
 
@@ -487,33 +530,75 @@
         igrad_ref[f] = (inner * root * live).astype(BF16)
         return 0
 
-    lax.fori_loop(0, frames, finish, 0)
+    lax.fori_loop(0, frames // 2, finish, 0)
+    stage0 = fourth_stage(0, stage0)
+    stage2 = third_stage(2, stage2)
+    lax.fori_loop(frames // 2, frames, finish, 0)
     igrad_copy = pltpu.make_async_copy(igrad_ref, igrad_hbm, local_sem.at[4])
     igrad_copy.start()
 
-    stage0 = fourth_stage(0, stage0)
-    stage2 = third_stage(2, stage2)
     stage1 = fourth_stage(1, stage1)
-    z_copy.wait()
-    pair_ref[...] = x_total[...] + z_sum[...]
+    for copy in x_copies:
+        copy.wait()
+    x_total[...] = x_sums[0] + x_sums[1] + x_sums[2] + x_sums[3]
+    z_copy = send(x_total, z_sum, pair_send.at[11], pair_recv.at[11], across)
     stage0 = fifth_stage(0, stage0)
     stage2 = fourth_stage(2, stage2)
     stage1 = fifth_stage(1, stage1)
+    z_copy.wait()
+    pair_ref[...] = x_total[...] + z_sum[...]
     stage2 = fifth_stage(2, stage2)
-    ends = [sixth_stage(0, stage0), sixth_stage(1, stage1), sixth_stage(2, stage2)]
-    for copy in ends:
-        copy.wait()
+    ends = (stage0, stage1, stage2)
+    for off in (1, 3, 2):
+        for k in range(3):
+            sixth_stage(k, off, ends[k])
+    outs = []
+    for k in range(3):
+        for copy in ends[k][1]:
+            copy.wait()
+        out = pltpu.make_async_copy(total_ref.at[k], total_hbm.at[k], local_sem.at[5 + k])
+        out.start()
+        outs.append(out)
     encoded_copy.wait()
     igrad_copy.wait()
 
     @pl.when(has_before)
     def _():
+        for f in range(frames):
+            moved(f).wait_send()
         halo.wait_send()
-        bulk.wait_send()
 
     @pl.when(has_after)
     def _():
         tails.wait_send()
+
+    for out in outs:
+        out.wait()
+
+
+def last_kernel(
+    scale, encoded_in, igrad_in, total_ref, pair_in,
+    encoded_out, igrad_out, kernel_ref, gain_ref, bias_ref, sem,
+):
+    step, steps = pl.program_id(0), pl.num_programs(0)
+    copies = [
+        pltpu.make_async_copy(encoded_in, encoded_out, sem.at[0]),
+        pltpu.make_async_copy(igrad_in, igrad_out, sem.at[1]),
+    ]
+
+    @pl.when(step == 0)
+    def _():
+        for copy in copies:
+            copy.start()
+        gain_ref[...] = pair_in[0:1] * scale
+        bias_ref[...] = pair_in[1:2] * scale
+
+    kernel_ref[...] = total_ref[...].astype(F32) * scale
+
+    @pl.when(step == steps - 1)
+    def _():
+        for copy in copies:
+            copy.wait()
 
 
 def body(loaded, lengths, resolution, weight, norm_gain, norm_bias, cotangent):
@@ -541,8 +626,9 @@
             shape((8, channels), F32),
         ),
         in_specs=[SMEM, SMEM, ANY, ANY, ANY, VMEM, VMEM],
-        out_specs=(ANY, ANY, VMEM, VMEM),
+        out_specs=(ANY, ANY, ANY, VMEM),
         scratch_shapes=[
+            pltpu.VMEM(slab, BF16),
             pltpu.VMEM(slab, BF16),
             pltpu.VMEM(slab, BF16),
             pltpu.VMEM(slab, BF16),
@@ -565,6 +651,8 @@
             pltpu.VMEM((slabs, 8, channels), F32),
             small,
             pltpu.VMEM((slabs, 8, channels), F32),
+            pltpu.VMEM((3, blocks, 16, channels), BF16),
+            tiles(3, blocks, kind=F32),
             tiles(3, blocks, kind=F32),
             tiles(3, blocks),
             tiles(3, blocks),
@@ -578,13 +666,13 @@
             pltpu.VMEM((4, 8, channels), F32),
             small,
             small,
-            dma((5,)),
-            dma((3,)),
-            dma((3,)),
+            dma((8,)),
+            dma((frames + 2,)),
+            dma((frames + 2,)),
             dma((7,)),
             dma((7,)),
-            dma((7, 3, 3)),
-            dma((7, 3, 3)),
+            dma((7, 3, 4)),
+            dma((7, 3, 4)),
             dma((12,)),
             dma((12,)),
         ],
@@ -599,13 +687,30 @@
         norm_bias.reshape(1, channels),
     )
     scale = 1.0 / math.sqrt(lax.axis_size("dp") * slabs * frames * places)
+    taps = pl.BlockSpec((3, channels, channels), lambda i: (i, 0, 0))
+    line = pl.BlockSpec((1, channels), lambda i: (0, 0))
+    encoded, igrad, kernel, gain, bias = pl.pallas_call(
+        functools.partial(last_kernel, scale),
+        out_shape=(
+            shape(slab, BF16),
+            shape(slab, BF16),
+            shape((27, channels, channels), F32),
+            shape((1, channels), F32),
+            shape((1, channels), F32),
+        ),
+        grid=(9,),
+        in_specs=[ANY, ANY, taps, pl.BlockSpec((8, channels), lambda i: (0, 0))],
+        out_specs=(ANY, ANY, taps, line, line),
+        scratch_shapes=[dma((2,))],
+        compiler_params=params(58),
+    )(encoded, igrad, total.reshape(27, channels, channels), pair)
     whole = (1, frames, rows, cols, channels)
     return (
         encoded.reshape(whole),
         igrad.reshape(whole),
-        total.reshape(27, channels, channels).astype(F32) * scale,
-        pair[0] * scale,
-        pair[1] * scale,
+        kernel,
+        gain.reshape(channels),
+        bias.reshape(channels),
     )
 
 

time: 102 us -> 166 us (1.63)
  Pallas kernels: 92.1 us -> 165 us
  other arithmetic: 7.41 us -> 0 us
  local copies, waits for them, and re-layouts: 1.95 us -> 0 us
    pallas_call x0 -> x1, Pallas kernels: none -> 66.5 us  [body(): pl.pallas_call(functools.partial(last_kernel, scale), out_shape=(shape(sl...]
    mul x2 -> x0, other arithmetic: 7.41 us -> none  [the longest x1 5.98 us: body(): total.reshape(27, channels, channels).astype(F32) * scale]
    pallas_call x1, Pallas kernels: 92.1 us -> 98.3 us  [body(): pl.pallas_call(functools.partial(section_kernel, rows, cols, width), out_...]
    unnamed x6 -> x0, local copies, waits for them, and re-layouts: 1.95 us -> none
where the time goes in v4:
time: 166 us
  Pallas kernels  165 us (99%)
    pallas_call x1, Pallas kernels, body(): pl.pallas_call(functools.partial(section_kernel, rows, cols, width), out_...  98.3 us
    pallas_call x1, Pallas kernels, body(): pl.pallas_call(functools.partial(last_kernel, scale), out_shape=(shape(sl...  66.5 us

profile of v4, /device:TPU:1, one launch (start us, length us, event | category | flops | bytes accessed | tf_op | source)
XLA Modules:
  0.0 165.6 jit_solution(8894623446196834085)
XLA Ops:
  0.6 98.3 %shard_map.110 = (bf16[8,256,256]{2,1,0:T(8,128)(2,1)}, bf16[8,256,256]{2,1,0:T(8,128)(2,1)}, bf16[3,144,16,256]{3,2,1,0:T(8,128)(2,1)}, f32[8,256]{1,0:T(8,128)}) custom-call(s32[1,8]{1,0:T(1,128)} %len_ref.1, s32[1,2]{1,0:T(1,128)} %res_ref.1, bf16[8,256,256]{2,1,0:T(8,128)(2,1)} %bitcast.12, bf16[8,256,256]{2,1,0:T(8,128)(2,1)} %bitcast.13, ...), custom_call_target="tpu_custom_call" | custom-call | tf_op jit(solution)/shard_map/pallas_call | solution.py:620
  98.9 66.5 %shard_map.111 = (bf16[8,256,256]{2,1,0:T(8,128)(2,1)}, bf16[8,256,256]{2,1,0:T(8,128)(2,1)}, f32[27,256,256]{2,1,0:T(8,128)}, f32[1,256]{1,0:T(1,128)}, f32[1,256]{1,0:T(1,128)}) custom-call(bf16[8,256,256]{2,1,0:T(8,128)(2,1)} %get-tuple-element.14.encoded_in, bf16[8,256,256]{2,1,0:T(8,128)(2,1)} %get-tuple-element.15.igrad_in, ...), custom_call_target="tpu_custom_call" | custom-call | tf_op jit(solution)/shard_map/pallas_call | solution.py:692

commit v5 on v4

--- a/solution.py
+++ b/solution.py
@@ -10,12 +10,13 @@
 
 GROUPS = 32
 EPSILON = 1e-05
+LIMIT = 45
 MESH = pl.DeviceIdType.MESH
 F32 = jnp.float32
 BF16 = jnp.bfloat16
 
 VMEM = pl.BlockSpec(memory_space=pltpu.VMEM)
-ANY = pl.BlockSpec(memory_space=pl.ANY)
+HBM = pl.BlockSpec(memory_space=pltpu.HBM)
 SMEM = pl.BlockSpec(memory_space=pltpu.SMEM)
 
 
@@ -71,12 +72,12 @@
 
 def section_kernel(
     rows, cols, width,
-    len_ref, res_ref, loaded_hbm, cot_hbm, weight_hbm, gain_ref, bias_ref,
-    encoded_hbm, igrad_hbm, total_hbm, pair_ref,
-    loaded_ref, leaving_ref, arrived_ref, cot_ref, next_ref, tail_out, tail_ref, weight_ref, turned_ref,
-    back_cat, cat_ref, grad_ref, agrad_ref, normed_ref, encoded_ref, igrad_ref,
+    len_ref, res_ref, loaded_ref, cot_ref, weight_hbm, gain_ref, bias_ref,
+    encoded_ref, igrad_ref, total_ref, pair_ref,
+    arrived_ref, next_ref, tail_out, tail_ref, weight_ref, turned_ref,
+    back_cat, cat_ref, grad_ref, agrad_ref, normed_ref,
     mask_ref, first_ref, last_ref, stats_out, stats_ref, sums_ref, slabs_ref,
-    total_ref, own_part, far_sum, far_part, core_in, send1, in1, send2, in2, in3,
+    own_part, far_sum, far_part, core_in, send1, in1, send2, in2, in3,
     tm_total, core_sum, x_sums, x_total, z_sum,
     local_sem, move_send, move_recv, stat_send, stat_recv,
     send_sem, recv_sem, pair_send, pair_recv,
@@ -113,14 +114,8 @@
     for peer in greeted:
         pl.semaphore_signal(barrier, inc=1, device_id=peer, device_id_type=MESH)
 
-    loads = [
-        pltpu.make_async_copy(src, dst, local_sem.at[i])
-        for i, (src, dst) in enumerate(
-            ((loaded_hbm, loaded_ref), (cot_hbm, cot_ref), (weight_hbm, weight_ref))
-        )
-    ]
-    for load in loads:
-        load.start()
+    load = pltpu.make_async_copy(weight_hbm, weight_ref, local_sem)
+    load.start()
 
     def remote(src, dst, send_at, recv_at, peer):
         return pltpu.make_async_remote_copy(
@@ -134,7 +129,7 @@
         return copy
 
     halo = remote(
-        cot_hbm.at[pl.ds(0, 2)], next_ref, move_send.at[frames], move_recv.at[frames], before
+        cot_ref.at[pl.ds(0, 2)], next_ref, move_send.at[frames], move_recv.at[frames], before
     )
     tails = remote(
         tail_out, tail_ref, move_send.at[frames + 1], move_recv.at[frames + 1], after
@@ -142,7 +137,7 @@
 
     def moved(f):
         return remote(
-            leaving_ref.at[f], arrived_ref.at[f], move_send.at[f], move_recv.at[f], before
+            igrad_ref.at[f], arrived_ref.at[f], move_send.at[f], move_recv.at[f], before
         )
 
     @pl.when(tm == slabs - 1)
@@ -165,7 +160,6 @@
     zero = jnp.zeros((8, channels), F32)
     row = lax.broadcasted_iota(jnp.int32, (8, channels), 0)
 
-    loads[0].wait()
 
     def fold(value):
         return jnp.sum(value.reshape(places // 8, 8, channels), axis=0)
@@ -200,7 +194,7 @@
         offset = (tm - 1) * frames + f - own_start
         usable = (offset >= 0) & (offset < own_length)
         picked = loaded_ref[jnp.clip(offset, 0, frames - 1)]
-        leaving_ref[f] = jnp.where(usable, picked, jnp.zeros_like(picked))
+        igrad_ref[f] = jnp.where(usable, picked, jnp.zeros_like(picked))
         return 0
 
     lax.fori_loop(0, frames, pack, 0)
@@ -217,11 +211,9 @@
 
     @pl.when(has_before)
     def _():
-        for f in range(frames):
-            moved(f).start()
-        halo.start()
-
-    loads[2].wait()
+        moved(0).start()
+
+    load.wait()
 
     def turn(block, _):
         for k in range(3):
@@ -241,7 +233,6 @@
         lay_out(back_cat, frame, value, rows, cols, first_ref[...], last_ref[...])
         return value
 
-    loads[1].wait()
 
     def own_grad(f, _):
         value = place(f, cot_ref[f])
@@ -263,10 +254,17 @@
         agrad_ref[f] = convolve(back_cat, turned_ref, f, True)
         return 0
 
-    lax.fori_loop(0, frames - 2, back_sweep, 0)
-
     for copy in stats_shares:
         copy.wait()
+
+    @pl.when(has_before)
+    def _():
+        for f in range(1, frames):
+            moved(f).start()
+        halo.start()
+
+    lax.fori_loop(0, frames - 2, back_sweep, 0)
+
     counts = [(len_ref[0, i] * area).astype(F32) for i in range(slabs)]
     mean = jnp.zeros((1, channels), F32)
     for i in range(slabs):
@@ -479,8 +477,6 @@
     half2 = kernel_part(2)
     stage1 = first_stage(1, half1)
     lax.fori_loop(early, frames, forward_sweep, 0)
-    encoded_copy = pltpu.make_async_copy(encoded_ref, encoded_hbm, local_sem.at[3])
-    encoded_copy.start()
     stage2 = first_stage(2, half2)
 
     @pl.when(has_after)
@@ -524,6 +520,11 @@
     shares_of = group_sum(tm_total[...] * gain, width) / count
     mean_part, along_part = shares_of[1:2], shares_of[0:1]
 
+    @pl.when(has_before)
+    def _():
+        for f in range(frames):
+            moved(f).wait_send()
+
     def finish(f, _):
         live = mask_ref[...] * (tm * frames + f < frame_total).astype(F32)
         inner = agrad_ref[f] - mean_part - normed_ref[f] * along_part
@@ -534,8 +535,6 @@
     stage0 = fourth_stage(0, stage0)
     stage2 = third_stage(2, stage2)
     lax.fori_loop(frames // 2, frames, finish, 0)
-    igrad_copy = pltpu.make_async_copy(igrad_ref, igrad_hbm, local_sem.at[4])
-    igrad_copy.start()
 
     stage1 = fourth_stage(1, stage1)
     for copy in x_copies:
@@ -552,53 +551,17 @@
     for off in (1, 3, 2):
         for k in range(3):
             sixth_stage(k, off, ends[k])
-    outs = []
     for k in range(3):
         for copy in ends[k][1]:
             copy.wait()
-        out = pltpu.make_async_copy(total_ref.at[k], total_hbm.at[k], local_sem.at[5 + k])
-        out.start()
-        outs.append(out)
-    encoded_copy.wait()
-    igrad_copy.wait()
 
     @pl.when(has_before)
     def _():
-        for f in range(frames):
-            moved(f).wait_send()
         halo.wait_send()
 
     @pl.when(has_after)
     def _():
         tails.wait_send()
-
-    for out in outs:
-        out.wait()
-
-
-def last_kernel(
-    scale, encoded_in, igrad_in, total_ref, pair_in,
-    encoded_out, igrad_out, kernel_ref, gain_ref, bias_ref, sem,
-):
-    step, steps = pl.program_id(0), pl.num_programs(0)
-    copies = [
-        pltpu.make_async_copy(encoded_in, encoded_out, sem.at[0]),
-        pltpu.make_async_copy(igrad_in, igrad_out, sem.at[1]),
-    ]
-
-    @pl.when(step == 0)
-    def _():
-        for copy in copies:
-            copy.start()
-        gain_ref[...] = pair_in[0:1] * scale
-        bias_ref[...] = pair_in[1:2] * scale
-
-    kernel_ref[...] = total_ref[...].astype(F32) * scale
-
-    @pl.when(step == steps - 1)
-    def _():
-        for copy in copies:
-            copy.wait()
 
 
 def body(loaded, lengths, resolution, weight, norm_gain, norm_bias, cotangent):
@@ -625,12 +588,9 @@
             shape((3, blocks, 16, channels), BF16),
             shape((8, channels), F32),
         ),
-        in_specs=[SMEM, SMEM, ANY, ANY, ANY, VMEM, VMEM],
-        out_specs=(ANY, ANY, ANY, VMEM),
+        in_specs=[SMEM, SMEM, VMEM, VMEM, HBM, VMEM, VMEM],
+        out_specs=(VMEM,) * 4,
         scratch_shapes=[
-            pltpu.VMEM(slab, BF16),
-            pltpu.VMEM(slab, BF16),
-            pltpu.VMEM(slab, BF16),
             pltpu.VMEM(slab, BF16),
             pltpu.VMEM((2, places, channels), BF16),
             pltpu.VMEM((2, places, channels), BF16),
@@ -642,8 +602,6 @@
             pltpu.VMEM((frames * places, channels), BF16),
             pltpu.VMEM(slab, F32),
             pltpu.VMEM(slab, F32),
-            pltpu.VMEM(slab, BF16),
-            pltpu.VMEM(slab, BF16),
             plane,
             plane,
             plane,
@@ -651,7 +609,6 @@
             pltpu.VMEM((slabs, 8, channels), F32),
             small,
             pltpu.VMEM((slabs, 8, channels), F32),
-            pltpu.VMEM((3, blocks, 16, channels), BF16),
             tiles(3, blocks, kind=F32),
             tiles(3, blocks, kind=F32),
             tiles(3, blocks),
@@ -666,7 +623,7 @@
             pltpu.VMEM((4, 8, channels), F32),
             small,
             small,
-            dma((8,)),
+            dma,
             dma((frames + 2,)),
             dma((frames + 2,)),
             dma((7,)),
@@ -676,7 +633,7 @@
             dma((12,)),
             dma((12,)),
         ],
-        compiler_params=params(58, collective_id=1, has_side_effects=True),
+        compiler_params=params(LIMIT, collective_id=1, has_side_effects=True),
     )(
         lengths,
         resolution,
@@ -687,30 +644,13 @@
         norm_bias.reshape(1, channels),
     )
     scale = 1.0 / math.sqrt(lax.axis_size("dp") * slabs * frames * places)
-    taps = pl.BlockSpec((3, channels, channels), lambda i: (i, 0, 0))
-    line = pl.BlockSpec((1, channels), lambda i: (0, 0))
-    encoded, igrad, kernel, gain, bias = pl.pallas_call(
-        functools.partial(last_kernel, scale),
-        out_shape=(
-            shape(slab, BF16),
-            shape(slab, BF16),
-            shape((27, channels, channels), F32),
-            shape((1, channels), F32),
-            shape((1, channels), F32),
-        ),
-        grid=(9,),
-        in_specs=[ANY, ANY, taps, pl.BlockSpec((8, channels), lambda i: (0, 0))],
-        out_specs=(ANY, ANY, taps, line, line),
-        scratch_shapes=[dma((2,))],
-        compiler_params=params(58),
-    )(encoded, igrad, total.reshape(27, channels, channels), pair)
     whole = (1, frames, rows, cols, channels)
     return (
         encoded.reshape(whole),
         igrad.reshape(whole),
-        kernel,
-        gain.reshape(channels),
-        bias.reshape(channels),
+        total.reshape(27, channels, channels).astype(F32) * scale,
+        pair[0] * scale,
+        pair[1] * scale,
     )
 
 

time: 166 us -> 95.1 us (0.57)
  Pallas kernels: 165 us -> 82.6 us
  local copies, waits for them, and re-layouts: 0 us -> 7.05 us
  other arithmetic: 0 us -> 4.55 us
    pallas_call x1 -> x0, Pallas kernels: 66.5 us -> none  [body(): pl.pallas_call(functools.partial(last_kernel, scale), out_shape=(shape(sl...]
    pallas_call x1, Pallas kernels: 98.3 us -> 82.6 us  [body(): pl.pallas_call(functools.partial(section_kernel, rows, cols, width), out_...]
    unnamed x0 -> x14, local copies, waits for them, and re-layouts: none -> 7.05 us
    mul x0 -> x2, other arithmetic: none -> 4.55 us  [the longest x1 3.98 us: body(): total.reshape(27, channels, channels).astype(F32) * scale]
where the time goes in v5:
time: 95.1 us; the launch traced here: 94.8 us
  Pallas kernels  82.6 us (87%)
  local copies, waits for them, and re-layouts  7.05 us (7%)
  other arithmetic  4.55 us (5%)
    pallas_call x1, Pallas kernels, body(): pl.pallas_call(functools.partial(section_kernel, rows, cols, width), out_...  82.6 us
    unnamed x14, local copies, waits for them, and re-layouts  7.05 us
    mul x1, other arithmetic, body(): total.reshape(27, channels, channels).astype(F32) * scale  3.98 us

profile of v5, /device:TPU:1, one launch (start us, length us, event | category | flops | bytes accessed | tf_op | source)
XLA Modules:
  0.0 94.8 jit_solution(12029977065793015659)
XLA Ops:
  0.6 0.0 copy-start
  0.6 1.2 %copy-done = bf16[1,8,16,16,256]{4,3,2,1,0:T(8,128)(2,1)S(1)} copy-done((bf16[1,8,16,16,256]{4,3,2,1,0:T(8,128)(2,1)S(1)}, bf16[1,8,16,16,256]{4,3,2,1,0:T(8,128)(2,1)}, u32[]{:S(2)}) %copy-start) | copy-done | bytes 1048600
  1.9 0.0 copy-start.1
  1.9 1.2 %copy-done.1 = bf16[1,8,16,16,256]{4,3,2,1,0:T(8,128)(2,1)S(1)} copy-done((bf16[1,8,16,16,256]{4,3,2,1,0:T(8,128)(2,1)S(1)}, bf16[1,8,16,16,256]{4,3,2,1,0:T(8,128)(2,1)}, u32[]{:S(2)}) %copy-start.1) | copy-done | bytes 1048600
  3.1 0.0 copy-start.2
  3.1 0.7 copy-done.2
  3.8 0.0 copy-start.3
  3.8 0.7 copy-done.3
  4.4 0.0 copy-start.4
  4.4 0.7 copy-done.4
  5.1 0.0 copy-start.5
  5.1 0.7 copy-done.5
  5.8 82.6 %shard_map.110 = (bf16[8,256,256]{2,1,0:T(8,128)(2,1)S(1)}, bf16[8,256,256]{2,1,0:T(8,128)(2,1)S(1)}, bf16[3,144,16,256]{3,2,1,0:T(8,128)(2,1)S(1)}, f32[8,256]{1,0:T(8,128)S(1)}) custom-call(s32[1,8]{1,0:T(1,128)S(1)} %copy-done.4, s32[1,2]{1,0:T(1,128)S(1)} %copy-done.5, bf16[8,256,256]{2,1,0:T(8,128)(2,1)S(1)} %bitcast.12, ...), custom_call_target="tpu_custom_call" | custom-call | tf_op jit(solution)/shard_map/pallas_call | solution.py:583
  88.3 0.6 slice_multiply_fusion
  88.9 4.0 %convert_multiply_fusion = f32[3,144,16,256]{3,2,1,0:T(8,128)} fusion(bf16[3,144,16,256]{3,2,1,0:T(8,128)(2,1)S(1)} %get-tuple-element.11), kind=kLoop, calls=%fused_computation | loop fusion | flops 3538944 | bytes 10616832 | tf_op jit(solution)/shard_map/mul | solution.py:651
  92.9 1.0 %copy.14 = bf16[1,8,16,16,256]{4,3,2,1,0:T(8,128)(2,1)} copy(bf16[1,8,16,16,256]{4,3,2,1,0:T(8,128)(2,1)S(1)} %bitcast.11) | data formatting | bytes 2097152
  93.9 1.0 %copy.15 = bf16[1,8,16,16,256]{4,3,2,1,0:T(8,128)(2,1)} copy(bf16[1,8,16,16,256]{4,3,2,1,0:T(8,128)(2,1)S(1)} %bitcast.10) | data formatting | bytes 2097152
Async XLA Ops:
  0.6 1.2 %copy-start = (bf16[1,8,16,16,256]{4,3,2,1,0:T(8,128)(2,1)S(1)}, bf16[1,8,16,16,256]{4,3,2,1,0:T(8,128)(2,1)}, u32[]{:S(2)}) copy-start(bf16[1,8,16,16,256]{4,3,2,1,0:T(8,128)(2,1)} %param.7) | copy-start | bytes 3145732
  1.9 1.2 %copy-start.1 = (bf16[1,8,16,16,256]{4,3,2,1,0:T(8,128)(2,1)S(1)}, bf16[1,8,16,16,256]{4,3,2,1,0:T(8,128)(2,1)}, u32[]{:S(2)}) copy-start(bf16[1,8,16,16,256]{4,3,2,1,0:T(8,128)(2,1)} %param.13) | copy-start | bytes 3145732
  3.1 0.7 copy-start.2
  3.8 0.7 copy-start.3
  4.4 0.7 copy-start.4
  5.1 0.7 copy-start.5

commit v6 on v5

--- a/solution.py
+++ b/solution.py
@@ -434,8 +434,29 @@
             return 0
 
         lax.fori_loop(0, piece // 3, add_third, 0)
-        spot = total_ref.at[k, pl.ds(base, piece), :, own_lanes]
-        return spread_out(4, k, order[k][1], lambda there: spot, lambda i: spot)
+        row_of = spread_out(
+            4, k, order[k][1],
+            lambda there: fragment(k, here[order[k][1]]),
+            lambda i: fragment(k, here[order[k][1]]),
+        )
+        return row_of, [hand_on(k, 0)]
+
+    def fragment(k, there):
+        base = here[order[k][0]] * part + there * piece
+        return total_ref.at[k, pl.ds(base, piece), :, own_lanes]
+
+    def hand_on(k, back):
+        spot = fragment(k, (here[order[k][1]] + 4 - back) % 4)
+        row_of = []
+        for off in (1, 2, 3):
+            at = 3 * back + off - 1
+            row_of.append(
+                send(
+                    spot, spot, send_sem.at[5, k, at], recv_sem.at[5, k, at],
+                    along(order[k][0], off)[1],
+                )
+            )
+        return row_of
 
     def region(k, there):
         return total_ref.at[k, pl.ds(there * part, part), :, own_lanes]
@@ -445,16 +466,15 @@
         return send(spot, spot, send_sem.at[6, k, i], recv_sem.at[6, k, i], other)
 
     def fifth_stage(k, copies):
-        for copy in copies:
-            copy.wait()
-        mine = here[order[k][0]]
-        row_of = spread_out(
-            5, k, order[k][0], lambda there: region(k, mine), lambda i: region(k, mine)
-        )
-        return row_of, [to_core(k, mine, 0)]
+        arriving, pieces = copies
+        for back in (1, 3, 2):
+            arriving[back - 1].wait()
+            pieces.append(hand_on(k, back))
+        return pieces, [to_core(k, here[order[k][0]], 0)]
 
     def sixth_stage(k, off, copies):
-        copies[0][off - 1].wait()
+        for row_of in copies[0]:
+            row_of[off - 1].wait()
         copies[1].append(to_core(k, (here[order[k][0]] + 4 - off) % 4, off))
 
     def forward_sweep(f, _):
@@ -476,8 +496,8 @@
     stage0 = first_stage(0, half0)
     half2 = kernel_part(2)
     stage1 = first_stage(1, half1)
+    stage2 = first_stage(2, half2)
     lax.fori_loop(early, frames, forward_sweep, 0)
-    stage2 = first_stage(2, half2)
 
     @pl.when(has_after)
     def _():
@@ -562,6 +582,10 @@
     @pl.when(has_after)
     def _():
         tails.wait_send()
+
+
+def pinned(value):
+    return pltpu.with_memory_space_constraint(value, pltpu.HBM)
 
 
 def body(loaded, lengths, resolution, weight, norm_gain, norm_bias, cotangent):
@@ -628,20 +652,25 @@
             dma((frames + 2,)),
             dma((7,)),
             dma((7,)),
-            dma((7, 3, 4)),
-            dma((7, 3, 4)),
+            dma((7, 3, 12)),
+            dma((7, 3, 12)),
             dma((12,)),
             dma((12,)),
         ],
         compiler_params=params(LIMIT, collective_id=1, has_side_effects=True),
     )(
-        lengths,
-        resolution,
-        loaded.reshape(slab),
-        cotangent.reshape(slab),
-        weight.reshape(9, 3 * channels, channels),
-        norm_gain.reshape(1, channels),
-        norm_bias.reshape(1, channels),
+        *map(
+            pinned,
+            (
+                lengths,
+                resolution,
+                loaded.reshape(slab),
+                cotangent.reshape(slab),
+                weight.reshape(9, 3 * channels, channels),
+                norm_gain.reshape(1, channels),
+                norm_bias.reshape(1, channels),
+            ),
+        )
     )
     scale = 1.0 / math.sqrt(lax.axis_size("dp") * slabs * frames * places)
     whole = (1, frames, rows, cols, channels)

time: 95.1 us -> 89.9 us (0.945)
  local copies, waits for them, and re-layouts: 7.05 us -> 1.94 us
    unnamed x14 -> x2, local copies, waits for them, and re-layouts: 7.05 us -> 1.94 us
where the time goes in v6:
time: 89.9 us; the launch traced here: 89.8 us
  Pallas kernels  82.7 us (92%)
  other arithmetic  4.55 us (5%)
  local copies, waits for them, and re-layouts  1.94 us (2%)
    pallas_call x1, Pallas kernels, body(): pl.pallas_call(functools.partial(section_kernel, rows, cols, width), out_...  82.7 us
    mul x1, other arithmetic, body(): total.reshape(27, channels, channels).astype(F32) * scale  3.98 us
    unnamed x2, local copies, waits for them, and re-layouts  1.94 us

profile of v6, /device:TPU:1, one launch (start us, length us, event | category | flops | bytes accessed | tf_op | source)
XLA Modules:
  0.0 89.8 jit_solution(1603152479304036042)
XLA Ops:
  0.6 82.7 %shard_map.110 = (bf16[8,256,256]{2,1,0:T(8,128)(2,1)S(1)}, bf16[8,256,256]{2,1,0:T(8,128)(2,1)S(1)}, bf16[3,144,16,256]{3,2,1,0:T(8,128)(2,1)S(1)}, f32[8,256]{1,0:T(8,128)S(1)}) custom-call(s32[1,8]{1,0:T(1,128)} %len_ref.1, s32[1,2]{1,0:T(1,128)} %res_ref.1, bf16[8,256,256]{2,1,0:T(8,128)(2,1)} %bitcast.14, bf16[8,256,256]{2,1,0:T(8,128)(2,1)} %bitcast.15, ...), custom_call_target="tpu_custom_call" | custom-call | tf_op jit(solution)/shard_map/pallas_call | solution.py:607
  83.3 0.6 slice_multiply_fusion
  83.9 4.0 %convert_multiply_fusion = f32[3,144,16,256]{3,2,1,0:T(8,128)} fusion(bf16[3,144,16,256]{3,2,1,0:T(8,128)(2,1)S(1)} %get-tuple-element.11), kind=kLoop, calls=%fused_computation | loop fusion | flops 3538944 | bytes 10616832 | tf_op jit(solution)/shard_map/mul | solution.py:680
  87.9 1.0 %copy.14 = bf16[1,8,16,16,256]{4,3,2,1,0:T(8,128)(2,1)} copy(bf16[1,8,16,16,256]{4,3,2,1,0:T(8,128)(2,1)S(1)} %bitcast.11) | data formatting | bytes 2097152
  88.8 1.0 %copy.15 = bf16[1,8,16,16,256]{4,3,2,1,0:T(8,128)(2,1)} copy(bf16[1,8,16,16,256]{4,3,2,1,0:T(8,128)(2,1)S(1)} %bitcast.10) | data formatting | bytes 2097152

commit v7 on v6

--- a/solution.py
+++ b/solution.py
@@ -212,6 +212,7 @@
     @pl.when(has_before)
     def _():
         moved(0).start()
+        moved(1).start()
 
     load.wait()
 
@@ -259,7 +260,7 @@
 
     @pl.when(has_before)
     def _():
-        for f in range(1, frames):
+        for f in range(2, frames):
             moved(f).start()
         halo.start()
 

time: 89.9 us -> 89.3 us (level)
  no operation moved by 1% of the time
where the time goes in v7:
time: 89.3 us; the launch traced here: 89.2 us
  Pallas kernels  82 us (92%)
  other arithmetic  4.55 us (5%)
  local copies, waits for them, and re-layouts  1.94 us (2%)
    pallas_call x1, Pallas kernels, body(): pl.pallas_call(functools.partial(section_kernel, rows, cols, width), out_...  82 us
    mul x1, other arithmetic, body(): total.reshape(27, channels, channels).astype(F32) * scale  3.98 us
    unnamed x2, local copies, waits for them, and re-layouts  1.94 us

profile of v7, /device:TPU:1, one launch (start us, length us, event | category | flops | bytes accessed | tf_op | source)
XLA Modules:
  0.0 89.2 jit_solution(2919678025379029024)
XLA Ops:
  0.6 82.0 %shard_map.110 = (bf16[8,256,256]{2,1,0:T(8,128)(2,1)S(1)}, bf16[8,256,256]{2,1,0:T(8,128)(2,1)S(1)}, bf16[3,144,16,256]{3,2,1,0:T(8,128)(2,1)S(1)}, f32[8,256]{1,0:T(8,128)S(1)}) custom-call(s32[1,8]{1,0:T(1,128)} %len_ref.1, s32[1,2]{1,0:T(1,128)} %res_ref.1, bf16[8,256,256]{2,1,0:T(8,128)(2,1)} %bitcast.14, bf16[8,256,256]{2,1,0:T(8,128)(2,1)} %bitcast.15, ...), custom_call_target="tpu_custom_call" | custom-call | tf_op jit(solution)/shard_map/pallas_call | solution.py:608
  82.7 0.6 slice_multiply_fusion
  83.3 4.0 %convert_multiply_fusion = f32[3,144,16,256]{3,2,1,0:T(8,128)} fusion(bf16[3,144,16,256]{3,2,1,0:T(8,128)(2,1)S(1)} %get-tuple-element.11), kind=kLoop, calls=%fused_computation | loop fusion | flops 3538944 | bytes 10616832 | tf_op jit(solution)/shard_map/mul | solution.py:681
  87.2 1.0 %copy.14 = bf16[1,8,16,16,256]{4,3,2,1,0:T(8,128)(2,1)} copy(bf16[1,8,16,16,256]{4,3,2,1,0:T(8,128)(2,1)S(1)} %bitcast.11) | data formatting | bytes 2097152
  88.2 1.0 %copy.15 = bf16[1,8,16,16,256]{4,3,2,1,0:T(8,128)(2,1)} copy(bf16[1,8,16,16,256]{4,3,2,1,0:T(8,128)(2,1)S(1)} %bitcast.10) | data formatting | bytes 2097152

commit v8 on v7

--- a/solution.py
+++ b/solution.py
@@ -487,7 +487,8 @@
         forward_sweep(f, 0)
         return 0
 
-    lax.fori_loop(0, early, take_in, 0)
+    lax.fori_loop(0, early - 1, take_in, 0)
+    lax.fori_loop(early - 1, early, own_frame, 0)
     for k in range(3):
         early_part(k)
     lax.fori_loop(early, frames, own_frame, 0)
@@ -498,7 +499,7 @@
     half2 = kernel_part(2)
     stage1 = first_stage(1, half1)
     stage2 = first_stage(2, half2)
-    lax.fori_loop(early, frames, forward_sweep, 0)
+    lax.fori_loop(early - 1, frames, forward_sweep, 0)
 
     @pl.when(has_after)
     def _():

time: 89.3 us -> 89.3 us (level)
  no operation moved by 1% of the time
where the time goes in v8:
time: 89.3 us; the launch traced here: 89.2 us
  Pallas kernels  82.1 us (92%)
  other arithmetic  4.55 us (5%)
  local copies, waits for them, and re-layouts  1.94 us (2%)
    pallas_call x1, Pallas kernels, body(): pl.pallas_call(functools.partial(section_kernel, rows, cols, width), out_...  82.1 us
    mul x1, other arithmetic, body(): total.reshape(27, channels, channels).astype(F32) * scale  3.98 us
    unnamed x2, local copies, waits for them, and re-layouts  1.94 us

profile of v8, /device:TPU:1, one launch (start us, length us, event | category | flops | bytes accessed | tf_op | source)
XLA Modules:
  0.0 89.2 jit_solution(15050159419115239117)
XLA Ops:
  0.6 82.1 %shard_map.110 = (bf16[8,256,256]{2,1,0:T(8,128)(2,1)S(1)}, bf16[8,256,256]{2,1,0:T(8,128)(2,1)S(1)}, bf16[3,144,16,256]{3,2,1,0:T(8,128)(2,1)S(1)}, f32[8,256]{1,0:T(8,128)S(1)}) custom-call(s32[1,8]{1,0:T(1,128)} %len_ref.1, s32[1,2]{1,0:T(1,128)} %res_ref.1, bf16[8,256,256]{2,1,0:T(8,128)(2,1)} %bitcast.14, bf16[8,256,256]{2,1,0:T(8,128)(2,1)} %bitcast.15, ...), custom_call_target="tpu_custom_call" | custom-call | tf_op jit(solution)/shard_map/pallas_call | solution.py:609
  82.7 0.6 slice_multiply_fusion
  83.3 4.0 %convert_multiply_fusion = f32[3,144,16,256]{3,2,1,0:T(8,128)} fusion(bf16[3,144,16,256]{3,2,1,0:T(8,128)(2,1)S(1)} %get-tuple-element.11), kind=kLoop, calls=%fused_computation | loop fusion | flops 3538944 | bytes 10616832 | tf_op jit(solution)/shard_map/mul | solution.py:682
  87.3 1.0 %copy.14 = bf16[1,8,16,16,256]{4,3,2,1,0:T(8,128)(2,1)} copy(bf16[1,8,16,16,256]{4,3,2,1,0:T(8,128)(2,1)S(1)} %bitcast.11) | data formatting | bytes 2097152
  88.2 1.0 %copy.15 = bf16[1,8,16,16,256]{4,3,2,1,0:T(8,128)(2,1)} copy(bf16[1,8,16,16,256]{4,3,2,1,0:T(8,128)(2,1)S(1)} %bitcast.10) | data formatting | bytes 2097152
